TPU v7x, 32 devices: a whole 2x2x4 slice. The times are simulated.
32 devices in a mesh: blk: 8 (over z, y), head: 4 (over x, core).
Axes of the slice: x: 2, y: 2, z: 4, core: 2. Of those that a mesh axis runs over, the one named last changes fastest.
Arguments:
- tokens: bfloat16 [2, 12288, 768], P(None, ('blk', 'head')), may hold values from -6 to 6
- w_query: bfloat16 [768, 768], P(('blk', 'head')), may hold values from -0.3125 to 0.3125
- w_key: bfloat16 [768, 768], P(('blk', 'head')), may hold values from -0.3125 to 0.3125
- w_value: bfloat16 [768, 768], P(('blk', 'head')), may hold values from -0.21875 to 0.21875
- w_out: bfloat16 [768, 768], P(('blk', 'head')), may hold values from -0.625 to 0.625
- conv_kernel: bfloat16 [12, 33], P('head'), may hold values from -0.5 to 0.5
- norm1_gain: bfloat16 [768], P(('blk', 'head')), may hold values from 0.25 to 1.75
- w_up: bfloat16 [768, 3072], P(('blk', 'head')), may hold values from -0.21875 to 0.21875
- w_down: bfloat16 [3072, 768], P(('blk', 'head')), may hold values from -0.21875 to 0.21875
- norm2_gain: bfloat16 [768], P(('blk', 'head')), may hold values from 0.25 to 1.75
- cotangent: bfloat16 [2, 12288, 768], P(None, ('blk', 'head')), may hold values from -6 to 6
Outputs:
- layer_out: bfloat16 [2, 12288, 768], P(None, ('blk', 'head'))
- grad_tokens: bfloat16 [2, 12288, 768], P(None, ('blk', 'head'))
- grad_query: float32 [768, 768], P(('blk', 'head'))
- grad_key: float32 [768, 768], P(('blk', 'head'))
- grad_value: float32 [768, 768], P(('blk', 'head'))
- grad_out: float32 [768, 768], P(('blk', 'head'))
- grad_conv: float32 [12, 33], P('head')
- grad_norm1: float32 [768], P(('blk', 'head'))
- grad_up: float32 [768, 3072], P(('blk', 'head'))
- grad_down: float32 [3072, 768], P(('blk', 'head'))
- grad_norm2: float32 [768], P(('blk', 'head'))
All inputs are finite; a program needn't handle non-finite values.
Results may differ from a plain program's by a relative error of at most 0.015.
The roundings to bfloat16 on the way count: a program that leaves them out, or rounds other values in their place, can miss the bound.
Values may be sent and summed in bfloat16 or wider, within the bound.
No kernel may reach another device: no remote copies, remote signals or barrier semaphores. Data moves between devices by JAX's collectives and lax.ppermute only.
A program may use at most 192 MiB of HBM per device.

v0:
```python
import functools

import jax
import jax.numpy as jnp
from jax import lax
from jax.experimental import pallas as pl
from jax.experimental.pallas import tpu as pltpu
from jax.sharding import PartitionSpec as P

HD = 64
M = 64
KW = 33
NEWTON = 6
REACH = KW // 2
AX = ("blk", "head")
EPS = 1e-05
GW = 256
HP = GW // HD
CT = 128
CE = CT + 2 * REACH

bf16 = jnp.bfloat16
f32 = jnp.float32
HIGHEST = lax.Precision.HIGHEST


def nn(a, b):
    return lax.dot_general(a, b, (((1,), (0,)), ((), ())), preferred_element_type=f32)


def nt(a, b):
    return lax.dot_general(a, b, (((1,), (1,)), ((), ())), preferred_element_type=f32)


def tn(a, b):
    return lax.dot_general(a, b, (((0,), (0,)), ((), ())), preferred_element_type=f32)


def exact(a, b, dims=((1,), (0,))):
    return lax.dot_general(a, b, (dims, ((), ())), preferred_element_type=f32, precision=HIGHEST)


def iota(shape, dim):
    return lax.broadcasted_iota(jnp.int32, shape, dim)


class Fetched:
    def __init__(self, source, buf, sems, parts):
        self.buf, self.shape, self.dtype = buf, buf.shape, buf.dtype
        self.copies = [
            pltpu.make_async_copy(source.at[part], buf.at[part], sem)
            for part, sem in zip(parts, sems)
        ]
        self.waiting = list(range(len(parts)))
        for copy in self.copies:
            copy.start()

    def ready(self, *which):
        for i in which or tuple(self.waiting):
            if i in self.waiting:
                self.copies[i].wait()
                self.waiting.remove(i)

    def __getitem__(self, index):
        self.ready()
        return self.buf[index]


class Stored:
    def __init__(self, target, buf, sems, parts):
        self.buf, self.shape, self.dtype = buf, buf.shape, buf.dtype
        self.copies = [
            pltpu.make_async_copy(buf.at[part], target.at[part], sem)
            for part, sem in zip(parts, sems)
        ]
        self.left = list(range(len(parts)))

    def done(self, *which):
        for i in which or tuple(self.left):
            if i in self.left:
                self.copies[i].start()
                self.left.remove(i)

    def __getitem__(self, index):
        return self.buf[index]

    def __setitem__(self, index, value):
        self.buf[index] = value


def ready(*refs):
    for ref in refs:
        if isinstance(ref, Fetched):
            ref.ready()


def done(*refs):
    for ref in refs:
        if isinstance(ref, Stored):
            ref.done()


def resident_call(kernel, outs, args):
    vmem = pl.BlockSpec(memory_space=pltpu.VMEM)
    return pl.pallas_call(
        kernel,
        out_shape=outs,
        in_specs=[vmem] * len(args),
        out_specs=jax.tree.map(lambda _: vmem, outs),
        compiler_params=pltpu.CompilerParams(vmem_limit_bytes=8 << 20),
    )(*args)


def vmem_call(kernel, outs, args, scalars=0, scratch=(), parts=None, out_parts=None, lent=None):
    lent = lent or {}
    parts, out_parts = parts or {}, out_parts or {}
    arrays = args[scalars:]
    whole = [(slice(None),)]
    pieces = [parts.get(i, whole) for i in range(len(arrays))]
    results = jax.tree.leaves(outs)
    own_results = [r for i, r in enumerate(results) if i not in lent]
    buffers = [pltpu.VMEM(a.shape, a.dtype) for a in [*arrays, *own_results]]
    out_pieces = [out_parts.get(i, whole) for i in range(len(results))]
    semaphores = pltpu.SemaphoreType.DMA((sum(len(p) for p in pieces + out_pieces),))

    def run(*refs):
        refs = list(refs)
        take = lambda k: [refs.pop(0) for _ in range(k)]
        ins, sources, targets = take(scalars), take(len(arrays)), take(len(results))
        kept, in_bufs, own_bufs = take(len(scratch)), take(len(arrays)), take(len(own_results))
        out_bufs = [
            in_bufs[lent[i]] if i in lent else own_bufs.pop(0) for i in range(len(results))
        ]
        (sems,) = refs
        free = iter(range(sum(len(p) for p in pieces + out_pieces)))
        own = lambda piece: [sems.at[next(free)] for _ in piece]
        for source, buf, piece in zip(sources, in_bufs, pieces):
            ins.append(Fetched(source, buf, own(piece), piece))
        stored = [
            Stored(target, buf, own(piece), piece)
            for target, buf, piece in zip(targets, out_bufs, out_pieces)
        ]
        kernel(*ins, *stored, *kept)
        ready(*ins)
        done(*stored)
        for ref in stored:
            for copy in ref.copies:
                copy.wait()

    hbm = pl.BlockSpec(memory_space=pl.ANY)
    return pl.pallas_call(
        run,
        out_shape=outs,
        in_specs=[pl.BlockSpec(memory_space=pltpu.SMEM)] * scalars + [hbm] * len(arrays),
        out_specs=jax.tree.map(lambda _: hbm, outs),
        scratch_shapes=list(scratch) + buffers + [semaphores],
        compiler_params=pltpu.CompilerParams(vmem_limit_bytes=60 << 20),
    )(*args)


def shape_of(dims, dtype):
    return jax.ShapeDtypeStruct(tuple(dims), dtype)


def cube_masks(n):
    masks = [1 << b for b in range(n.bit_length() - 1)]
    if len(masks) >= 2:
        masks[-1] |= masks[-2]
    return masks


def coefficients(v, n):
    bits = [(v >> b) & 1 for b in range(n.bit_length() - 1)]
    if len(bits) >= 2:
        bits[-2] = bits[-2] ^ bits[-1]
    return bits


def scatter_order(n, core, turn):
    rest = [b for b in range(n.bit_length() - 1) if b != core]
    return (rest, [rest[1], rest[0], *rest[2:]], [*rest[2:], *rest[:2]])[turn]


def gather_order(n, core, turn):
    return list(reversed(scatter_order(n, core, turn)))


def swap(x, n, dim):
    mask = cube_masks(n)[dim]
    return lax.ppermute(x, AX, [(i, i ^ mask) for i in range(n)])


def gather_slot(v, n, core, turn):
    bits = coefficients(v, n)
    slot = 0
    for place, dim in enumerate(gather_order(n, core, turn)):
        slot = slot + (bits[dim] << place)
    return slot


def scatter_slot(v, n, core, turn):
    bits = coefficients(v, n)
    slot = 0
    for place, dim in enumerate(reversed(scatter_order(n, core, turn))):
        slot = slot + (bits[dim] << place)
    return slot


def cube_gather(piece, n, core):
    buf = piece[None]
    first, second = gather_order(n, core, 0), gather_order(n, core, 1)
    for dim in first[:-2]:
        buf = jnp.concatenate([buf, swap(buf, n, dim)], axis=0)
    half = piece.shape[1] // 2
    mid = buf
    bufs = [buf[:, :, :half], buf[:, :, half:]]
    for dims in zip(first[-2:], second[-2:]):
        got = [swap(x, n, dim) for x, dim in zip(bufs, dims)]
        bufs = [jnp.concatenate(pair, axis=0) for pair in zip(bufs, got)]
    return bufs + [swap(x, n, core) for x in bufs], mid


def merged(jobs, call):
    shapes = []
    for pairs in jobs:
        slots = pairs[0][0].shape[0]
        joint = (sum(k.shape[1] for k, _ in pairs), pairs[0][0].shape[2])
        shapes += [shape_of((slots // 2,) + joint, t) for t in (f32, bf16)]
    args = [x for pairs in jobs for pair in pairs for x in pair]
    kernel = functools.partial(merge_kernel, [len(pairs) for pairs in jobs])
    outs = call(kernel, shapes, args)
    return list(zip(outs[0::2], outs[1::2]))


def cube_scatter(jobs, splits, n, core):
    orders = [[core, *scatter_order(n, core, turn)] for turn in range(len(jobs))]
    jobs = [[(k, swap(s, n, core)) for k, s in job] for job in jobs]
    for step in range(1, len(orders[0])):
        state = merged(jobs, vmem_call if step == 1 else resident_call)
        if step == 3:
            orders = orders[:1] + orders[2:]
        jobs = [[(k, swap(s, n, o[step]))] for (k, s), o in zip(state, orders)]
        if step == 2:
            jobs = [jobs[0] + jobs[1]] + jobs[2:]
    width = jobs[0][0][0].shape[2]
    shapes = [shape_of((count, width), f32) for split in splits for count in split]
    args = [x for pairs in jobs for pair in pairs for x in pair]
    return resident_call(functools.partial(last_kernel, splits), shapes, args)


def emit(acc, first_row, rows, stride, keep, send, rows_at, me, n, core, turn, count=None, first=0):
    count = n if count is None else count
    mine = me & 1
    span = slice(rows_at, rows_at + rows)

    def step(i, c):
        d = 2 * i
        slot = scatter_slot(jnp.bitwise_xor(me - mine, first + d), n, core, turn)
        low = pl.multiple_of(first_row + (d + mine) * stride, 8)
        high = pl.multiple_of(first_row + (d + 1 - mine) * stride, 8)
        keep[slot, span, :] = acc[pl.ds(low, rows), :].astype(bf16)
        send[slot, span, :] = acc[pl.ds(high, rows), :].astype(bf16)
        return c

    lax.fori_loop(0, count // 2, step, 0)


def aligned(i, size):
    return pl.ds(pl.multiple_of(i * size, size), size)


def block_mask():
    return (iota((GW, GW), 0) // HD) == (iota((GW, GW), 1) // HD)


def block_diagonal(x):
    wide = jnp.concatenate([x] * HP, axis=0)
    return jnp.where(block_mask(), wide, jnp.zeros_like(wide))


def diagonal_half(x, j):
    return x[j * HD : (j + 1) * HD, 128 * (j // 2) : 128 * (j // 2) + 128]


def low_lanes(x, j):
    return pltpu.roll(x, HD, 1) if j % 2 else x


def high_lanes(x, j):
    return x if j % 2 else pltpu.roll(x, HD, 1)


SLOT = HD // 2 + 8


def packed(x):
    half = HD // 2
    lane = iota((half, 128), 1)
    return jnp.where(lane < HD, x[0:half], pltpu.roll(x[half:HD], HD, 1))


def unpacked(x):
    half = HD // 2
    both = jnp.concatenate([x[0:half], pltpu.roll(x[0:half], HD, 1)], axis=0)
    return jnp.where(iota((HD, 128), 1) < HD, both, 0.0)


def stacked(rows, height=8):
    rows = list(rows) + [jnp.zeros_like(rows[0])] * (height - len(rows))
    return jnp.concatenate(rows, axis=0)


def identity(size):
    return (iota((size, size), 0) == iota((size, size), 1)).astype(bf16)


def block_from_slots(read):
    rows = []
    for j in range(HP):
        half = unpacked(read(j).astype(f32))
        if j % 2:
            half = pltpu.roll(half, HD, 1)
        zero = jnp.zeros_like(half)
        rows.append(jnp.concatenate([half, zero] if j < 2 else [zero, half], axis=1))
    return jnp.concatenate(rows, axis=0).astype(bf16)


def prepare_kernel(chunks, taps_ref, gains_ref, wq, wk, wv, wo, wu, wd, now_ref, later_ref, ext):
    rows, width = wq.shape
    heads_dev, reach = taps_ref.shape
    ext[...] = jnp.zeros_like(ext)
    ext[0:heads_dev, 0:reach] = taps_ref[...].astype(f32)
    back = (iota((128, 128), 0) + iota((128, 128), 1) == KW - 1).astype(bf16)
    turned = nn(ext[...].astype(bf16), back)
    ext[heads_dev : 2 * heads_dev, :] = turned[0:heads_dev]
    ext[6:8, 0:rows] = gains_ref[...].astype(f32)
    for i, w in enumerate((wq, wk, wv)):
        now_ref[i * rows : (i + 1) * rows, :] = w[...]
    now_ref[3 * rows : 3 * rows + 8, 0:128] = ext[...].astype(bf16)
    now_ref[3 * rows : 3 * rows + 8, 128:] = jnp.zeros((8, width - 128), bf16)
    done(now_ref)
    later_ref[0 : chunks * rows, :] = wd[...]
    for k in range(chunks):
        at = (chunks + k) * rows
        later_ref[at : at + rows, :] = wu[:, k * width : (k + 1) * width]
    later_ref[2 * chunks * rows : (2 * chunks + 1) * rows, :] = wo[...]


def piece_pair(ins, turn, pair, span, lanes, me, n, core):
    mine = me & 1
    slot = gather_slot(jnp.bitwise_xor(me - mine, 2 * pair), n, core, turn)
    own = ins[turn][slot, span, lanes]
    other = ins[2 + turn][slot, span, lanes]
    return jnp.where(mine == 0, own, other), jnp.where(mine == 0, other, own)


def natural(ins, units, me, n, core, rows, width):
    half = width // 2

    def place_rows(pair, c):
        to = pl.ds(pl.multiple_of(2 * rows * pair, 16), 2 * rows)
        for turn in range(2):
            for unit, out in units:
                span = slice(unit * rows, (unit + 1) * rows)
                both = piece_pair(ins, turn, pair, span, slice(None), me, n, core)
                out[to, turn * half : (turn + 1) * half] = jnp.concatenate(both, axis=0)
        return c

    lax.fori_loop(0, n // 2, place_rows, 0)


def query_key_kernel(cfg, me_ref, x_ref, *refs):
    n, core, hyper, rows, parts, scale, segment, heads_dev, head_size = cfg
    ins, refs = refs[:4], refs[4:]
    q_ref, k_ref, land_ref, wqk = refs
    me = me_ref[0]
    width = x_ref.shape[1]
    ready(*ins)
    if hyper:
        natural(ins, ((0, wqk.buf.at[0]), (1, wqk.buf.at[1])), me, n, core, rows, width)
    else:
        for unit, piece in enumerate(ins[:2]):
            wqk[unit] = piece[...]
    done(wqk)
    q_ref[...] = (nn(x_ref[...], wqk[0]) * scale).astype(bf16)
    done(q_ref)
    k_ref[...] = (nn(x_ref[...], wqk[1]) * scale).astype(bf16)
    done(k_ref)
    pieces = []
    each = x_ref.shape[0] // (2 * parts)
    for ref in (q_ref, k_ref):
        for at_row in range(2 * parts):
            span = ref[at_row * each : (at_row + 1) * each, :].astype(f32)
            pieces.append(jnp.sum(span, axis=0, keepdims=True) * (1.0 / segment))
    if parts < 2:
        pieces.append(jnp.zeros((8 - 4 * parts, width), f32))
    shared = jnp.concatenate(pieces, axis=0).astype(land_ref.dtype)
    for d in range(n):
        land_ref[d] = shared


def value_kernel(cfg, me_ref, x_ref, *refs):
    n, core, hyper, rows, parts, scale, segment, heads_dev, head_size = cfg
    ins, refs = refs[:4], refs[4:]
    v_ref, toep_ref, peot_ref, gain_ref, wv = refs
    me = me_ref[0]
    width = x_ref.shape[1]
    ready(*ins)
    if hyper:
        natural(ins, ((2, wv),), me, n, core, rows, width)

        def small_pair(pair):
            span = slice(3 * rows, 3 * rows + 8)
            return piece_pair(ins, 0, pair, span, slice(0, GW), me, n, core)

    else:
        wv[...] = ins[2][...]

        def small_pair(pair):
            return ins[3][2 * pair, :, 0:GW], ins[3][2 * pair + 1, :, 0:GW]

    done(wv)
    v_ref[...] = nn(x_ref[...], wv[...]).astype(bf16)
    done(v_ref)
    place = (iota((128, width), 1) % rows == iota((128, width), 0)).astype(bf16)

    def add(d, small, gains):
        inside = iota((8, width), 1) // rows == d
        return gains + jnp.where(inside, nn(small[:, 0:128], place), 0.0)

    def add_pair(pair, gains):
        first, second = small_pair(pair)
        return add(2 * pair + 1, second, add(2 * pair, first, gains))

    gain_ref[...] = lax.fori_loop(0, n // 2, add_pair, jnp.zeros(gain_ref.shape, f32))
    for d in range(head_size):
        taps = small_pair(d // 2)[d % 2].astype(f32)
        for i in range(heads_dev):
            for row, out in ((i, toep_ref), (heads_dev + i, peot_ref)):
                spread = jnp.broadcast_to(taps[row : row + 1, :], (CT, GW))
                spread = pltpu.roll(spread, 0, 1, stride=1, stride_axis=0)
                out[d * heads_dev + i] = spread[:, 0:CE].astype(bf16)


def newton_kernel(heads, me_ref, ql_ref, kl_ref, inv_ref, keep_ref, two_ref):
    unit = lax.rem(me_ref[0], 2 * heads)
    second = unit >= heads
    head = jnp.where(second, unit - heads, unit)
    width = ql_ref.shape[1]
    pick = (iota((width, HD), 0) == iota((width, HD), 1) + head * HD).astype(bf16)

    def mine(ref):
        rows = jnp.where(second, ref[M : 2 * M, :].astype(f32), ref[0:M, :].astype(f32))
        return nn(rows.astype(bf16), pick).astype(bf16)

    query, key = mine(ql_ref), mine(kl_ref)
    score = nt(query, key)
    e = jnp.exp(score - jnp.max(score, axis=1, keepdims=True))
    kernel = e / jnp.sum(e, axis=1, keepdims=True)
    column = jnp.sum(kernel, axis=0, keepdims=True)
    largest = jnp.max(column, axis=1, keepdims=True)
    eye = (iota((M, M), 0) == iota((M, M), 1)).astype(f32)
    z = kernel.T / largest
    two_ref[0] = kernel
    two_ref[1] = column + jnp.zeros_like(kernel)
    two_ref[2] = query.astype(f32)
    two_ref[3] = key.astype(f32)

    def iterate(step, z):
        p = exact(kernel, z)
        a = 7.0 * eye - p
        b = 15.0 * eye - exact(p, a)
        c = 13.0 * eye - exact(p, b)
        for i, value in enumerate((z, p, a, b, c)):
            keep_ref[step, i] = value
        return 0.25 * exact(z, c)

    inv_ref[...] = lax.fori_loop(0, NEWTON, iterate, z)


def newton_back_kernel(
    heads, me_ref, dinv_ref, inv_ref, keep_ref, two_ref, dq_ref, dk_ref
):
    turned = ((0,), (0,))
    across = ((1,), (1,))
    ready(keep_ref)
    kernel = two_ref[0]

    def iterate(i, state):
        dz, dkernel = state
        step = NEWTON - 1 - i
        z, p, a, b, c = (keep_ref[step, k] for k in range(5))
        dc = 0.25 * exact(z, dz, turned)
        db = -exact(p, dc, turned)
        da = -exact(p, db, turned)
        dp = -exact(dc, b, across) - exact(db, a, across) - da
        dkernel = dkernel + exact(dp, z, across)
        return 0.25 * exact(dz, c, across) + exact(kernel, dp, turned), dkernel

    dz, dkernel = lax.fori_loop(0, NEWTON, iterate, (dinv_ref[...], jnp.zeros_like(kernel)))
    column = two_ref[1]
    largest = jnp.max(column[0:1, :], axis=1, keepdims=True)
    dkernel = dkernel + dz.T / largest
    dlargest = -jnp.sum(dz * kernel.T, keepdims=True) / (largest * largest)
    top = (column == largest).astype(f32)
    ties = jnp.sum(top[0:1, :], axis=1, keepdims=True)
    dkernel = dkernel + dlargest * top / ties
    dscore = kernel * (dkernel - jnp.sum(dkernel * kernel, axis=1, keepdims=True))
    dquery = exact(dscore, two_ref[3])
    dkey = exact(dscore, two_ref[2], turned)
    unit = me_ref[0]
    width = dq_ref.shape[2]
    second = lax.rem(unit, 2 * heads) >= heads
    head = jnp.where(second, unit - heads, unit)
    place = (iota((HD, width), 1) == iota((HD, width), 0) + head * HD).astype(f32)
    live = unit < 2 * heads
    for out, value in ((dq_ref, dquery), (dk_ref, dkey)):
        wide = exact(jnp.where(live, value, 0.0), place)
        out[0] = jnp.where(second, 0.0, wide)
        out[1] = jnp.where(second, wide, 0.0)


def score3_kernel(heads, parts, k_ref, v_ref, got_ref, ql_ref, kl_ref, p_ref, out_ref, lands):
    tokens = k_ref.shape[0] // 2
    n = out_ref.shape[0]
    width = k_ref.shape[1]
    ready(got_ref)
    for d in range(n):
        got = got_ref[d].astype(f32)
        for i in range(4):
            lands[i, d * parts : (d + 1) * parts, :] = got[i * parts : (i + 1) * parts]
    for i, out in ((0, ql_ref), (2, kl_ref)):
        both = lands[i : i + 2]
        if n * parts != M:
            both = jnp.sum(both.reshape(2, M, n * parts // M, width), axis=2)
        out[...] = both.reshape(2 * M, width).astype(bf16)
    for u in range(2 * heads, n):
        out_ref[u] = jnp.zeros((SLOT, 128), bf16)
    ready(k_ref, v_ref)
    done(ql_ref, kl_ref)

    @pl.loop(0, 2)
    def _(s):
        for g in range(k_ref.shape[1] // GW):
            lanes = slice(g * GW, (g + 1) * GW)
            rows = aligned(s, tokens)
            land = block_diagonal(ql_ref[aligned(s, M), lanes])
            score = nt(land, k_ref[rows, lanes])
            top = jnp.max(score, axis=1, keepdims=True).astype(bf16).astype(f32)
            e = jnp.exp(score - top)
            total = jnp.sum(e, axis=1, keepdims=True)
            low = e.astype(bf16)
            p_ref[s, g] = low
            part = nn(low, v_ref[rows, lanes])
            high = total.astype(bf16).astype(f32)
            which = iota((GW, 8), 1)
            stats = jnp.where(which == 0, top, 0.0)
            stats = jnp.where(which == 1, high, stats)
            stats = jnp.where(which == 2, total - high, stats).astype(bf16)
            stats = tn(stats, identity(GW))
            for j in range(HP):
                slot = packed(low_lanes(diagonal_half(part, j), j))
                stat = low_lanes(stats[:, 128 * (j // 2) : 128 * (j // 2) + 128], j)
                slot = jnp.concatenate([slot, stat], axis=0)
                out_ref[s * heads + g * HP + j] = slot.astype(bf16)


def combine_kernel(got_ref, inv_ref, out_ref, sum_ref):
    n = got_ref.shape[0]
    half = HD // 2
    ready(got_ref)
    tops = jnp.concatenate([got_ref[d, half : half + 8].astype(f32)[0:1] for d in range(n)], axis=0)
    top = jnp.max(tops, axis=0, keepdims=True)
    weights = jnp.exp(tops - top)
    sums = []
    for d in range(n):
        stat = got_ref[d, half : half + 8].astype(f32)
        sums.append(stat[1:2] + stat[2:3])
    total = jnp.sum(weights * jnp.concatenate(sums, axis=0), axis=0, keepdims=True)
    total = jnp.where(total > 0.0, total, 1.0)
    weights = (weights / total).T
    lane = iota((half, 128), 1)
    acc = jnp.zeros((half, 128), f32)
    for d in range(n):
        by = weights[:, d : d + 1]
        by = jnp.where(lane < HD, by[0:half], by[half:HD])
        acc = acc + by * got_ref[d, 0:half].astype(f32)
    summary = unpacked(acc)
    sum_ref[...] = summary
    mixed = exact(inv_ref[...], summary)
    high = total.astype(bf16).astype(f32)
    slot = jnp.concatenate([packed(mixed), stacked([top, high, total - high])], axis=0)
    slot = slot.astype(bf16)
    for d in range(n):
        out_ref[d] = slot


def fill_extended(ext, ref, low_ref, high_ref, tokens):
    for s in range(2):
        ext[s, 0:REACH, :] = low_ref[s]
        ext[s, REACH : REACH + tokens, :] = ref[s * tokens : (s + 1) * tokens, :]
        ext[s, REACH + tokens : 2 * REACH + tokens, :] = high_ref[s]


def convolve(ext, toep_ref, s, g, tile):
    piece = ext[s, tile * CT : tile * CT + CE, aligned(g, GW)]
    lane = iota((CT, GW), 1) // HD
    out = nn(toep_ref[g * HP], piece)
    for j in range(1, HP):
        out = jnp.where(lane == j, nn(toep_ref[g * HP + j], piece), out)
    return out


def softmax1(land, queries):
    tokens = queries.shape[0]
    score = nt(land, queries).reshape(HP, M, tokens)
    e = jnp.exp(score - jnp.max(score, axis=1, keepdims=True))
    return (e / jnp.sum(e, axis=1, keepdims=True)).reshape(GW, tokens)


def kernel1_kernel(q_ref, v_ref, low_ref, high_ref, kl_ref, toep_ref, conv_ref, k1_ref, ext):
    tokens = q_ref.shape[0] // 2
    fill_extended(ext, v_ref, low_ref, high_ref, tokens)
    ready(q_ref, kl_ref, toep_ref)

    @pl.loop(0, 2)
    def _(s):
        for g in range(q_ref.shape[1] // GW):
            lanes = slice(g * GW, (g + 1) * GW)
            rows = aligned(s, tokens)
            land = block_diagonal(kl_ref[aligned(s, M), lanes])
            k1_ref[s, g] = softmax1(land, q_ref[rows, lanes]).astype(bf16)
            for tile in range(tokens // CT):
                at = pl.ds(pl.multiple_of(s * tokens + tile * CT, CT), CT)
                conv_ref[at, lanes] = convolve(ext, toep_ref, s, g, tile)


def norm(h):
    center = h - jnp.mean(h, axis=1, keepdims=True)
    rstd = lax.rsqrt(jnp.mean(center * center, axis=1, keepdims=True) + EPS)
    return center * rstd, rstd


def norm_back(dx, hat, rstd):
    return rstd * (
        dx - jnp.mean(dx, axis=1, keepdims=True) - hat * jnp.mean(dx * hat, axis=1, keepdims=True)
    )


RT = 128


def row_tiles(total, body):
    def step(i, c):
        body(pl.ds(pl.multiple_of(i * RT, RT), RT))
        return c

    lax.fori_loop(0, total // RT, step, 0, unroll=2)


def layer_kernel(chunks, heads, k1_ref, conv_ref, mixed_ref, x_ref, gain_ref, cot_ref, *refs):
    scratch, refs = refs[-9:], refs[:-9]
    heads_ref, act, du, n1b, dd, db, hat1, rstd1, acc = scratch
    hyper = len(refs) == 7
    weights, refs = (refs[:1], refs[1:]) if hyper else (refs[:3], refs[3:])
    mbd_ref, out_ref, dh1_ref, dheads_ref, gn_ref = refs[:5]
    grads = refs[5:]
    total, width = x_ref.shape
    tokens = total // 2

    if hyper:
        (fetched,) = weights
        all_ref = fetched.buf
        n, _, rows, _ = all_ref.shape
        per = n // chunks

        def w_up(c):
            return all_ref[:, chunks + c].reshape(width, width)

        def w_down(c):
            return all_ref[pl.ds(c * per, per), 0:chunks].reshape(width, width)

        def w_out():
            return all_ref[:, 2 * chunks].reshape(width, width)

        def put_up(c, g):
            all_ref[:, chunks + c] = g.reshape(n, rows, width)

        def put_down(c, g):
            all_ref[pl.ds(c * per, per), 0:chunks] = g.reshape(per, chunks, rows, width)

        def put_out(g):
            all_ref[:, 2 * chunks] = g.reshape(n, rows, width)

        out_ready, up_ready, down_ready = (functools.partial(fetched.ready, i) for i in range(3))
        out_done, up_done, down_done = (functools.partial(grads[0].done, i) for i in range(3))
    else:
        wo_ref, wu_ref, wd_ref = (w.buf for w in weights)
        w_up = lambda c: wu_ref[c]
        w_down = lambda c: wd_ref[c]
        w_out = lambda: wo_ref[...]

        def put_up(c, g):
            wu_ref[c] = g

        def put_down(c, g):
            wd_ref[c] = g

        def put_out(g):
            wo_ref[...] = g

        out_ready, up_ready, down_ready = (w.ready for w in weights)
        out_done, up_done, down_done = (g.done for g in grads)

    ready(k1_ref, conv_ref, mixed_ref)
    down = conv_ref.buf

    @pl.loop(0, 2)
    def _(s):
        for g in range(width // GW):
            lanes = slice(g * GW, (g + 1) * GW)
            span = aligned(s, tokens)
            mbd = block_from_slots(lambda j: mixed_ref[s * heads + g * HP + j, 0 : HD // 2])
            mbd_ref[s, g] = mbd
            heads_ref[span, lanes] = (tn(k1_ref[s, g], mbd) + down[span, lanes]).astype(bf16)

    done(mbd_ref)
    ready(gain_ref)
    g1 = gain_ref[6:7, :]
    g2 = gain_ref[7:8, :]
    gn_ref[...] = jnp.zeros(gn_ref.shape, f32)
    out_ready()
    ready(x_ref)
    down[...] = nn(heads_ref[...], w_out())

    def first(r):
        hat, rstd = norm(x_ref[r, :].astype(f32) + down[r, :])
        hat1[r, :] = hat
        rstd1[r, :] = jnp.broadcast_to(rstd, (RT, 128))
        value = hat * g1
        n1b[r, :] = value.astype(bf16)
        down[r, :] = value

    row_tiles(total, first)
    up_ready()
    down_ready()
    ready(cot_ref)

    @pl.loop(0, chunks)
    def _(c):
        up = nn(n1b[...], w_up(c))
        cdf = 0.5 * (1.0 + lax.erf(up * (0.5**0.5)))
        density = jnp.exp(-0.5 * up * up) * 0.3989422804014327
        value = (up * cdf).astype(bf16)
        act[c] = value
        du[c] = (cdf + up * density).astype(bf16)
        down[...] += nn(value, w_down(c))

    dh2 = dh1_ref.buf

    def second(r):
        hat, rstd = norm(down[r, :])
        out_ref[r, :] = (hat * g2).astype(bf16)
        g = cot_ref[r, :].astype(f32)
        gn_ref[1:2, :] += jnp.sum(g * hat, axis=0, keepdims=True)
        d = norm_back(g * g2, hat, rstd)
        dh2[r, :] = d
        dd[r, :] = d.astype(bf16)

    row_tiles(total, second)
    done(out_ref)

    @pl.loop(0, chunks)
    def _(c):
        part = (nt(dd[...], w_down(c)) * du[c].astype(f32)).astype(bf16)
        du[c] = part
        dh2[...] += nt(part, w_up(c))

    def third(r):
        hat = hat1[r, :]
        d = dh2[r, :]
        gn_ref[0:1, :] += jnp.sum(d * hat, axis=0, keepdims=True)
        d = norm_back(d * g1, hat, rstd1[r, :][:, 0:1])
        dh2[r, :] = d
        db[r, :] = d.astype(bf16)

    row_tiles(total, third)
    done(dh1_ref, gn_ref)
    dheads_ref[...] = nt(db[...], w_out()).astype(bf16)
    done(dheads_ref)

    @pl.loop(0, chunks)
    def _(c):
        acc[...] = tn(act[c], dd[...])
        put_down(c, acc[...].astype(bf16))

    down_done()

    @pl.loop(0, chunks)
    def _(c):
        acc[...] = tn(n1b[...], du[c])
        put_up(c, acc[...].astype(bf16))

    up_done()
    acc[...] = tn(heads_ref[...], db[...])
    put_out(acc[...].astype(bf16))
    out_done()


def attend_back_kernel(heads, dh_ref, k1_ref, mbd_ref, kl_ref, q_ref, dq_ref, dkl_ref, out_ref):
    tokens = q_ref.shape[0] // 2
    n = out_ref.shape[0]
    for u in range(2 * heads, n):
        out_ref[u] = jnp.zeros((HD // 2, 128), bf16)
    mask = block_mask()
    ready(dh_ref, k1_ref, mbd_ref, kl_ref, q_ref)

    @pl.loop(0, 2)
    def _(s):
        for g in range(q_ref.shape[1] // GW):
            lanes = slice(g * GW, (g + 1) * GW)
            rows = aligned(s, tokens)
            dh = dh_ref[rows, lanes]
            land = block_diagonal(kl_ref[aligned(s, M), lanes])
            low = k1_ref[s, g]
            k1 = low.astype(f32)
            dk1 = nt(mbd_ref[s, g], dh)
            row = jnp.sum((k1 * dk1).reshape(HP, M, tokens), axis=1, keepdims=True)
            centered = (dk1.reshape(HP, M, tokens) - row).reshape(GW, tokens)
            ds = (k1 * centered).astype(bf16)
            dq_ref[rows, lanes] = tn(ds, land)
            dland = jnp.where(mask, nn(ds, q_ref[rows, lanes]), 0.0)
            dkl_ref[s, :, lanes] = jnp.sum(dland.reshape(HP, M, GW), axis=0)
            dmixed = nn(low, dh)
            for j in range(HP):
                slot = packed(low_lanes(diagonal_half(dmixed, j), j))
                out_ref[s * heads + g * HP + j] = slot.astype(bf16)


def conv_back_kernel(
    dh_ref, dlow_ref, dhigh_ref, v_ref, low_ref, high_ref, peot_ref, dv_ref, gc_ref, dext, ext, gram
):
    tokens = v_ref.shape[0] // 2
    groups = v_ref.shape[1] // GW
    fill_extended(dext, dh_ref, dlow_ref, dhigh_ref, tokens)
    fill_extended(ext, v_ref, low_ref, high_ref, tokens)
    ready(peot_ref)
    lane = iota((CT, GW), 1) // HD
    ready(dh_ref)
    back = (iota((CT, CT), 0) + iota((CT, CT), 1) == CT - 1).astype(f32)

    @pl.loop(0, groups)
    def _(g):
        lanes = aligned(g, GW)
        gram[...] = jnp.zeros_like(gram)

        @pl.loop(0, 2)
        def _(s):
            for tile in range(tokens // CT):
                at = pl.ds(pl.multiple_of(s * tokens + tile * CT, CT), CT)
                dv_ref[at, lanes] = convolve(dext, peot_ref, s, g, tile)
                dh = dh_ref[at, lanes]
                each = jnp.concatenate(
                    [jnp.where(lane == j, dh, jnp.zeros_like(dh)) for j in range(HP)], axis=0
                )
                gram[:, 0:CE] += nt(each, ext[s, tile * CT : tile * CT + CE, lanes])

        rows = []
        for j in range(HP):
            turned = exact(back, gram[j * CT : (j + 1) * CT, :])
            rolled = pltpu.roll(turned, 0, 1, stride=1, stride_axis=0)
            rows.append(jnp.sum(rolled, axis=0, keepdims=True))
        gc_ref[g] = jnp.concatenate(rows, axis=0)


def owner_back_kernel(got_ref, inv_ref, sum_ref, out_ref, dinv_ref):
    n = got_ref.shape[0]
    ready(got_ref)
    dmixed = unpacked(
        lax.fori_loop(
            0, n, lambda d, a: a + got_ref[d].astype(f32), jnp.zeros((HD // 2, 128), f32)
        )
    )
    dsum = exact(inv_ref[...], dmixed, ((0,), (0,))).astype(bf16).astype(f32)
    ones = jnp.ones((8, 128), f32)
    row = exact(ones, dsum * sum_ref[...], ((1,), (1,)))[0:1]
    row = jnp.concatenate([row, jnp.zeros_like(row)], axis=1)
    high = row.astype(bf16).astype(f32)
    slot = jnp.concatenate([packed(dsum), stacked([high, row - high])], axis=0).astype(bf16)
    for d in range(n):
        out_ref[d] = slot
    done(out_ref)
    dinv_ref[...] = exact(dmixed, sum_ref[...], ((1,), (1,)))


def score3_back_kernel(
    heads, parts, sent_ref, stat_ref, dsum_ref, p_ref, k_ref, v_ref, ql_ref, dq2_ref, dk2_ref,
    dk1_ref, dk_ref, dv_ref, out_ref, dql,
):
    tokens = k_ref.shape[0] // 2
    n = out_ref.shape[0]
    mask = block_mask()
    ready(sent_ref, stat_ref, dsum_ref, p_ref, k_ref, v_ref, ql_ref, dq2_ref)

    @pl.loop(0, 2)
    def _(s):
        for g in range(k_ref.shape[1] // GW):
            lanes = slice(g * GW, (g + 1) * GW)
            rows = aligned(s, tokens)
            factors, terms = [], []
            for j in range(HP):
                u = s * heads + g * HP + j
                stat_rows = slice(HD // 2, HD // 2 + 8)
                local = sent_ref[u, stat_rows].astype(f32)[0:1]
                stat = stat_ref[u, stat_rows].astype(f32)
                factors.append(jnp.exp(local - stat[0:1]) / (stat[1:2] + stat[2:3]))
                d = dsum_ref[u, stat_rows].astype(f32)
                terms.append(d[0:1] + d[1:2])

            def joined(parts):
                lane = iota((1, 128), 1)
                halves = [
                    jnp.where(lane < HD, parts[j], pltpu.roll(parts[j + 1], HD, 1))
                    for j in range(0, HP, 2)
                ]
                return jnp.concatenate(halves, axis=1)

            rows_in = []
            for value in (joined(factors), joined(terms)):
                for _ in range(3):
                    term = value.astype(bf16).astype(f32)
                    rows_in.append(term)
                    value = value - term
            columns = nt(identity(GW), stacked(rows_in).astype(bf16))
            factor = columns[:, 0:1] + columns[:, 1:2] + columns[:, 2:3]
            term = columns[:, 3:4] + columns[:, 4:5] + columns[:, 5:6]
            k3 = p_ref[s, g].astype(f32) * factor
            dbd = block_from_slots(lambda j: dsum_ref[s * heads + g * HP + j, 0 : HD // 2])
            dk3 = nt(dbd, v_ref[rows, lanes])
            ds = (k3 * (dk3 - term)).astype(bf16)
            dland = jnp.where(mask, nn(ds, k_ref[rows, lanes]), 0.0)
            dql[s, :, lanes] = jnp.sum(dland.reshape(HP, M, GW), axis=0) + dq2_ref[s, :, lanes]
            land = block_diagonal(ql_ref[aligned(s, M), lanes])
            dk_ref[rows, lanes] = tn(ds, land)
            dv_ref[rows, lanes] = tn(k3.astype(bf16), dbd)
    for d in range(n):
        first = d * parts * M // (n * parts)
        span = slice(first, first + parts)
        pieces = [dql[0, span, :], dql[1, span, :]]
        pieces += [dk2_ref[s, span, :] + dk1_ref[s, span, :] for s in range(2)]
        if parts < 2:
            pieces.append(jnp.zeros((8 - 4 * parts, dql.shape[2]), f32))
        out_ref[d] = jnp.concatenate(pieces, axis=0).astype(bf16)


def two_terms(x):
    high = x.astype(bf16)
    return high, (x - high.astype(f32)).astype(bf16)


def final_kernel(
    cfg, me_ref, x_ref, dv3_ref, dvc_ref, dk3_ref, dq1_ref, wv, wqk, dh1_ref,
    dx_ref, sums_ref, gqk_ref, *refs
):
    n, core, hyper, rows, parts, scale, segment = cfg
    outs, acc, low, dv = refs[:-3], *refs[-3:]
    tokens = x_ref.shape[0] // 2
    each = tokens // parts
    dv[...] = (dvc_ref[...] + dv3_ref[...]).astype(bf16)
    acc[...] = tn(x_ref[...], dv[...])
    if hyper:
        emit(acc, 0, rows, rows, outs[0], outs[1], 0, me_ref[0], n, core, 2)
    else:
        outs[0][...] = acc[...]
    done(*outs)
    for s in range(2):
        for l in range(parts):
            span = slice(s * tokens + l * each, s * tokens + (l + 1) * each)
            at = s * parts + l
            sums_ref[at : at + 1, :] = jnp.sum(
                x_ref[span, :].astype(f32), axis=0, keepdims=True
            )
    done(sums_ref)
    low[1] = dk3_ref[...].astype(bf16)
    low[0] = dq1_ref[...].astype(bf16)
    ready(wqk, wv, dh1_ref)
    acc[...] = dh1_ref[...] + nt(dv[...], wv[...])

    @pl.loop(0, 2)
    def _(t):
        gqk_ref[t] = tn(x_ref[...], low[t]) * scale
        acc[...] += nt(low[t], wqk[t]) * scale

    dx_ref[...] = acc[...]


def landmark_sums(got_ref, factor):
    ready(got_ref)
    n, _, width = got_ref.shape
    zero = jnp.zeros((8, width), f32)
    return factor * lax.fori_loop(0, n, lambda d, a: a + got_ref[d].astype(f32), zero)


def landmark_kernel(cfg, me_ref, got_ref, sums_ref, gqk_ref, small_ref, *refs):
    n, core, hyper, rows, parts, scale, segment = cfg
    outs, acc = refs[:-1], refs[-1]
    me = me_ref[0]
    count = 2 * parts
    land = landmark_sums(got_ref, scale / segment)
    s_high, s_low = two_terms(sums_ref[0:count, :])
    left = jnp.concatenate([s_high, s_low, s_high], axis=0)
    for turn, base in enumerate((0, count)):
        high, low = two_terms(land[base : base + count, :])
        acc[...] = gqk_ref[turn] + tn(left, jnp.concatenate([high, high, low], axis=0))
        if hyper:
            keep, send = outs[2 * turn : 2 * turn + 2]
            emit(acc, 0, rows, rows, keep, send, 0, me, n, core, turn)
        else:
            outs[turn][...] = acc[...]
    if hyper:
        ready(small_ref)
        mine = me & 1
        span = slice(rows, rows + 8)

        def step(i, c):
            slot = scatter_slot(jnp.bitwise_xor(me - mine, 2 * i), n, core, 0)
            outs[0][slot, span, 0:GW] = small_ref[2 * i + mine]
            outs[1][slot, span, 0:GW] = small_ref[2 * i + 1 - mine]
            return c

        lax.fori_loop(0, n // 2, step, 0)


def tokens_kernel(cfg, got_ref, wqk, dx_ref, out_ref):
    n, core, hyper, rows, parts, scale, segment = cfg
    tokens = dx_ref.shape[0] // 2
    each = tokens // parts
    count = 2 * parts
    land = landmark_sums(got_ref, scale / segment)
    change = 0.0
    for turn, base in enumerate((0, count)):
        both = nt(jnp.concatenate(two_terms(land[base : base + count, :]), axis=0), wqk[turn])
        change = change + both[0:count] + both[count : 2 * count]
    for s in range(2):
        for l in range(parts):
            span = slice(s * tokens + l * each, s * tokens + (l + 1) * each)
            at = s * parts + l
            out_ref[span, :] = (dx_ref[span, :] + change[at : at + 1, :]).astype(bf16)


def merge_kernel(counts, *refs):
    ready(*refs[: 2 * sum(counts)])
    outs = refs[2 * sum(counts) :]
    at = 0
    for job, count in enumerate(counts):
        ins = refs[2 * at : 2 * (at + count)]
        at += count
        row = 0
        kept, sent = outs[2 * job], outs[2 * job + 1]
        for keep, got in zip(ins[0::2], ins[1::2]):
            span = slice(row, row + keep.shape[1])
            row += keep.shape[1]
            half = keep.shape[0] // 2

            @pl.loop(0, half)
            def _(j):
                kept[j, span] = keep[j].astype(f32) + got[j].astype(f32)
                sent[j, span] = (
                    keep[half + j].astype(f32) + got[half + j].astype(f32)
                ).astype(bf16)

        done(sent)


def last_kernel(splits, *refs):
    ins, outs = refs[: 2 * len(splits)], list(refs[2 * len(splits) :])
    for i, split in enumerate(splits):
        keep, got = ins[2 * i], ins[2 * i + 1]
        row = 0
        for count in split:
            span = slice(row, row + count)
            outs.pop(0)[...] = keep[0, span].astype(f32) + got[0, span].astype(f32)
            row += count


def unpack_kernel(chunks, got_ref, up_ref, down_ref, out_ref):
    out_ref[...] = got_ref[2 * chunks].astype(f32)
    rows, width = got_ref.shape[1:]
    for c in range(chunks):
        up_ref[:, c * width : (c + 1) * width] = got_ref[chunks + c].astype(f32)
        down_ref[c * rows : (c + 1) * rows, :] = got_ref[c].astype(f32)


def exchange(x):
    return lax.all_to_all(x, AX, 0, 0, tiled=True)


def per_device(
    tokens, w_query, w_key, w_value, w_out, conv_kernel, norm1_gain, w_up, w_down, norm2_gain, cotangent
):
    sequences, held, width = tokens.shape
    blk, head = lax.axis_size("blk"), lax.axis_size("head")
    n = blk * head
    heads_dev = conv_kernel.shape[0]
    heads = heads_dev * head
    rows = w_query.shape[0]
    hidden = w_up.shape[1]
    chunks = hidden // width
    segment = held * n // M
    parts = max(1, held // segment)
    groups = width // GW
    hyper = rows % 8 == 0 and n == 32
    core = 0 if n <= 32 else head.bit_length() - 1
    scale = HD**-0.25
    total = sequences * held
    me = (lax.axis_index("blk") * head + lax.axis_index("head")).astype(jnp.int32)
    me = me.reshape(1)
    x = tokens.reshape(total, width)

    if hyper:
        now, later = vmem_call(
            functools.partial(prepare_kernel, chunks),
            (
                shape_of((3 * rows + 8, width), bf16),
                shape_of(((2 * chunks + 1) * rows, width), bf16),
            ),
            (
                conv_kernel, jnp.stack([norm1_gain, norm2_gain]),
                w_query, w_key, w_value, w_out, w_up, w_down,
            ),
            scratch=[pltpu.VMEM((8, 128), f32)],
        )
        pieces, mid = cube_gather(now, n, core)
        later, _ = lax.optimization_barrier((later, mid))
        later = lax.all_gather(later, AX, axis=0).reshape(n, 2 * chunks + 1, rows, width)
        weights = (later,)
        weight_parts = {
            6: [
                (slice(None), slice(2 * chunks, None)),
                (slice(None), slice(chunks, 2 * chunks)),
                (slice(None), slice(0, chunks)),
            ]
        }
    else:
        taps = jnp.concatenate([conv_kernel, conv_kernel[:, ::-1]], axis=0)
        both = jnp.stack([norm1_gain, norm2_gain])
        extras = jnp.concatenate(
            [
                jnp.pad(taps, ((0, 0), (0, width - KW))),
                jnp.pad(both, ((0, 0), (0, width - rows))),
            ],
            axis=0,
        )
        pieces = [
            lax.all_gather(w, AX, axis=0, tiled=True) for w in (w_query, w_key, w_value)
        ] + [lax.all_gather(extras, AX, axis=0)]
        wo = lax.all_gather(w_out, AX, axis=0, tiled=True)
        wu = lax.all_gather(w_up, AX, axis=0, tiled=True)
        wu = wu.reshape(width, chunks, width).transpose(1, 0, 2)
        wd = lax.all_gather(w_down, AX, axis=0, tiled=True).reshape(chunks, width, width)
        weights = (wo, wu, wd)
        weight_parts = None

    cfg = (n, core, hyper, rows, parts, scale, segment, heads_dev, head)
    square_low = shape_of((total, width), bf16)
    square_full = shape_of((total, width), f32)
    weight = shape_of((width, width), bf16)
    weight_full = shape_of((width, width), f32)
    toeplitz = shape_of((heads, CT, CE), bf16)
    queries, keys, lands, wqk = vmem_call(
        functools.partial(query_key_kernel, cfg),
        (
            square_low, square_low, shape_of((n, 8, width), bf16 if held >= segment else f32),
            shape_of((2, width, width), bf16),
        ),
        (me, x, *pieces),
        scalars=1,
    )
    lands = exchange(lands)
    values, toep, peot, gains, wv = vmem_call(
        functools.partial(value_kernel, cfg),
        (square_low, toeplitz, toeplitz, shape_of((8, width), f32), weight),
        (me, x, *pieces),
        scalars=1,
    )
    lands, values = lax.optimization_barrier((lands, values))
    ahead = [(i, i + 1) for i in range(n - 1)]
    behind = [(i + 1, i) for i in range(n - 1)]

    def halo(y):
        y = y.reshape(sequences, held, width)
        low = lax.ppermute(y[:, held - REACH :], AX, ahead)
        high = lax.ppermute(y[:, :REACH], AX, behind)
        return low, high

    matrix = shape_of((M, M), f32)
    slots = shape_of((n, SLOT, 128), bf16)
    half_slots = shape_of((n, HD // 2, 128), bf16)
    land = shape_of((2 * M, width), bf16)
    q_land, k_land, p3, sent = vmem_call(
        functools.partial(score3_kernel, heads, parts),
        (land, land, shape_of((2, groups, GW, held), bf16), slots),
        (keys, values, lands),
        scratch=[pltpu.VMEM((4, n * parts, width), f32)],
    )
    got_sums = exchange(sent)
    inverse, newton_keep, kernel_two = vmem_call(
        functools.partial(newton_kernel, heads),
        (matrix, shape_of((NEWTON, 5, M, M), f32), shape_of((4, M, M), f32)),
        (me, q_land, k_land),
        scalars=1,
    )
    stat, summary = vmem_call(
        combine_kernel, (slots, shape_of((M, 128), f32)), (got_sums, inverse)
    )
    stat = exchange(stat)
    v_low, v_high = halo(values)
    convolved, k1 = vmem_call(
        kernel1_kernel,
        (square_full, shape_of((2, groups, GW, held), bf16)),
        (queries, values, v_low, v_high, k_land, toep),
        scratch=[pltpu.VMEM((2, held + 2 * REACH, width), bf16)],
    )
    stat, k1 = lax.optimization_barrier((stat, k1))
    wide = pltpu.VMEM((chunks, total, width), bf16)
    low_buffer = pltpu.VMEM((total, width), bf16)
    if hyper:
        grad_shapes = [shape_of((n, 2 * chunks + 1, rows, width), bf16)]
        grad_parts, lent = {5: weight_parts[6]}, {5: 6}
    else:
        grad_shapes = [shape_of(w.shape, bf16) for w in weights]
        grad_parts, lent = None, {5: 6, 6: 7, 7: 8}
    mbd, layer_out, d_h1, d_heads, gain_sums, *grads = vmem_call(
        functools.partial(layer_kernel, chunks, heads),
        [
            shape_of((2, groups, GW, GW), bf16), square_low, square_full, square_low,
            shape_of((8, width), f32),
        ]
        + grad_shapes,
        (k1, convolved, stat, x, gains, cotangent.reshape(total, width), *weights),
        scratch=[
            low_buffer, wide, wide, low_buffer, low_buffer, low_buffer,
            pltpu.VMEM((total, width), f32),
            pltpu.VMEM((total, 128), f32),
            pltpu.VMEM((width, width), f32),
        ],
        parts=weight_parts,
        out_parts=grad_parts,
        lent=lent,
    )
    d_low, d_high = halo(d_heads)
    spread = shape_of((2, M, width), f32)
    d_q1, d_kl1, sent_back = vmem_call(
        functools.partial(attend_back_kernel, heads),
        (square_full, spread, half_slots),
        (d_heads, k1, mbd, k_land, queries),
    )
    got_back = exchange(sent_back)
    extended = pltpu.VMEM((2, held + 2 * REACH, width), bf16)
    d_vc, conv_sums = vmem_call(
        conv_back_kernel,
        (square_full, shape_of((groups, HP, GW), f32)),
        (d_heads, d_low, d_high, values, v_low, v_high, peot),
        scratch=[extended, extended, pltpu.VMEM((HP * CT, GW), f32)],
    )
    got_back, d_vc = lax.optimization_barrier((got_back, d_vc))
    d_sum, d_inverse = vmem_call(
        owner_back_kernel, (slots, matrix), (got_back, inverse, summary)
    )
    d_sum = exchange(d_sum)
    d_ql2, d_kl2 = vmem_call(
        functools.partial(newton_back_kernel, heads),
        (spread, spread),
        (me, d_inverse, inverse, newton_keep, kernel_two),
        scalars=1,
    )
    d_k3, d_v3, sent_land = vmem_call(
        functools.partial(score3_back_kernel, heads, parts),
        (square_full, square_full, shape_of((n, 8, width), bf16)),
        (sent, stat, d_sum, p3, keys, values, q_land, d_ql2, d_kl2, d_kl1),
        scratch=[pltpu.VMEM((2, M, width), f32)],
    )
    got_land = exchange(sent_land)
    if hyper:
        early = lax.psum_scatter(grads[0], AX, scatter_dimension=0, tiled=False)
    small = gain_sums[0:2].reshape(2, n, rows).transpose(1, 0, 2).reshape(n, 2 * rows)
    tap_sums = conv_sums[:, :, CT - 1 : CT - 1 + KW].reshape(head, heads_dev * KW)
    tap_sums = jnp.broadcast_to(tap_sums[None], (blk, head, heads_dev * KW)).reshape(n, -1)
    small = jnp.concatenate([small, tap_sums], axis=1)
    small = jnp.pad(small, ((0, 0), (0, GW - small.shape[1])))
    extra_rows = (8, 0, 0)
    if hyper:
        slot_shapes = [
            [shape_of((n // 2, rows + extra, width), bf16)] * 2 for extra in extra_rows
        ]
    else:
        slot_shapes = [[shape_of((width, width), f32)]] * 3
    final_cfg = (n, core, hyper, rows, parts, scale, segment)
    d_x, x_sums, g_both, *value_slots = vmem_call(
        functools.partial(final_kernel, final_cfg),
        [square_full, shape_of((8, width), f32), shape_of((2, width, width), f32)] + slot_shapes[2],
        (me, x, d_v3, d_vc, d_k3, d_q1, wv, wqk, d_h1),
        scalars=1,
        scratch=[
            pltpu.VMEM((width, width), f32),
            pltpu.VMEM((2, total, width), bf16),
            pltpu.VMEM((total, width), bf16),
        ],
    )
    projections = vmem_call(
        functools.partial(landmark_kernel, final_cfg),
        slot_shapes[0] + slot_shapes[1],
        (
            me, got_land, x_sums, g_both,
            jnp.broadcast_to(small[:, None], (n, 8, GW)).astype(bf16),
        ),
        scalars=1,
        scratch=[pltpu.VMEM((width, width), f32)],
    )
    projections = list(projections) + value_slots
    after, _ = lax.optimization_barrier((got_land, projections))
    d_tokens = vmem_call(
        functools.partial(tokens_kernel, final_cfg), square_low, (after, wqk, d_x)
    )
    d_tokens = d_tokens.reshape(tokens.shape)
    if hyper:
        grad_up, grad_down, grad_out = vmem_call(
            functools.partial(unpack_kernel, chunks),
            (
                shape_of((rows, hidden), f32), shape_of((chunks * rows, width), f32),
                shape_of((rows, width), f32),
            ),
            (early,),
        )
        grad_query, small, grad_key, grad_value = cube_scatter(
            [
                [(projections[0], projections[1])],
                [(projections[2], projections[3])],
                [(projections[4], projections[5])],
            ],
            ((rows, 8, rows), (rows,)),
            n,
            core,
        )
        small = small[0]
    else:

        def scatter(g):
            return lax.psum_scatter(g, AX, scatter_dimension=0, tiled=True)

        grad_out = scatter(grads[0].astype(f32))
        grad_up = scatter(grads[1].astype(f32).transpose(1, 0, 2).reshape(width, hidden))
        grad_down = scatter(grads[2].astype(f32).reshape(hidden, width))
        grad_query, grad_key, grad_value = (scatter(g) for g in projections)
        small = scatter(small)[0]
    return (
        layer_out.reshape(tokens.shape),
        d_tokens,
        grad_query,
        grad_key,
        grad_value,
        grad_out,
        small[2 * rows : 2 * rows + heads_dev * KW].reshape(heads_dev, KW),
        small[:rows],
        grad_up,
        grad_down,
        small[rows : 2 * rows],
    )


def solution(mesh):
    lined = P(None, AX, None)
    rowed = P(AX, None)
    gain = P(AX)
    taps = P("head", None)
    in_specs = (lined, rowed, rowed, rowed, rowed, taps, gain, rowed, rowed, gain, lined)
    out_specs = (lined, lined, rowed, rowed, rowed, rowed, taps, gain, rowed, rowed, gain)
    return jax.shard_map(
        per_device, mesh=mesh, in_specs=in_specs, out_specs=out_specs, check_vma=False
    )
```

profile of v0, /device:TPU:0, one launch (start us, length us, event | category | flops | bytes accessed | tf_op | source)
XLA Modules:
  0.0 348.3 jit_solution(7106753415855464895)
XLA Ops:
  10.4 5.1 %collective-permute-start = (bf16[1,80,768]{2,1,0:T(8,128)(2,1)}, bf16[1,80,768]{2,1,0:T(8,128)(2,1)S(1)}, u32[]{:S(2)}, u32[]{:S(2)}) collective-permute-start(bf16[1,80,768]{2,1,0:T(8,128)(2,1)} %bitcast.28), channel_id=1, source_target_pairs={{0,24},{1,25},{2,26},{3,27},{4,28},{5,29},{6,30},{7,31},{8,16},{9,... | collective-permute-start | bytes 368648 | tf_op jit(solution)/shard_map/ppermute | solution.py:190
  22.4 5.3 %collective-permute-done.1 = bf16[2,80,768]{2,1,0:T(8,128)(2,1)S(1)} collective-permute-done((bf16[2,80,768]{2,1,0:T(8,128)(2,1)S(1)}, bf16[2,80,768]{2,1,0:T(8,128)(2,1)S(1)}, u32[]{:S(2)}, u32[]{:S(2)}) %collective-permute-start.1) | collective-permute-done | bytes 245792 | tf_op jit(solution)/shard_map/ppermute | solution.py:190
  38.4 11.0 %collective-permute-done.3 = bf16[8,80,384]{2,1,0:T(8,128)(2,1)S(1)} collective-permute-done((bf16[8,80,384]{2,1,0:T(8,128)(2,1)S(1)}, bf16[8,80,384]{2,1,0:T(8,128)(2,1)S(1)}, u32[]{:S(2)}, u32[]{:S(2)}) %collective-permute-start.3) | collective-permute-done | bytes 491552 | tf_op jit(solution)/shard_map/ppermute | solution.py:190
  53.7 6.1 %shard_map.195 = (bf16[768,768]{1,0:T(8,128)(2,1)}, bf16[768,768]{1,0:T(8,128)(2,1)}, bf16[32,8,768]{2,1,0:T(8,128)(2,1)}, bf16[2,768,768]{2,1,0:T(8,128)(2,1)}) custom-call(s32[1]{0:T(128)} %bitcast.refs_0_, bf16[768,768]{1,0:T(8,128)(2,1)} %bitcast.20, bf16[16,80,384]{2,1,0:T(8,128)(2,1)} %copy-done.3, bf16[16,80,384]{2,1,0:T(8,128)(2,1)} %copy-done.4, ...), custom_call_target="tpu_custom_call" | custom-call | tf_op jit(solution)/shard_map/pallas_call | solution.py:151
  63.9 8.3 %shard_map.196 = (bf16[768,768]{1,0:T(8,128)(2,1)}, bf16[12,128,160]{2,1,0:T(8,128)(2,1)}, bf16[12,128,160]{2,1,0:T(8,128)(2,1)}, f32[8,768]{1,0:T(8,128)}, bf16[768,768]{1,0:T(8,128)(2,1)}) custom-call(s32[1]{0:T(128)} %bitcast.refs_0_, bf16[768,768]{1,0:T(8,128)(2,1)} %bitcast.21, bf16[16,80,384]{2,1,0:T(8,128)(2,1)} %copy-done.3, ...), custom_call_target="tpu_custom_call" | custom-call | tf_op jit(solution)/shard_map/pallas_call | solution.py:151
  72.3 11.1 %all-to-all-done.refs_2_ = bf16[32,8,768]{2,1,0:T(8,128)(2,1)S(1)} async-done(((bf16[32,8,768]{2,1,0:T(8,128)(2,1)}), bf16[32,8,768]{2,1,0:T(8,128)(2,1)S(1)}, u32[]{:S(2)}, u32[]{:S(2)}) %all-to-all-start) | async-done | bytes 393248 | tf_op jit(solution)/shard_map/all_to_all | solution.py:1095
  84.2 6.2 %shard_map.197 = (bf16[128,768]{1,0:T(8,128)(2,1)}, bf16[128,768]{1,0:T(8,128)(2,1)}, bf16[2,3,256,384]{3,2,1,0:T(8,128)(2,1)}, bf16[32,40,128]{2,1,0:T(8,128)(2,1)}) custom-call(bf16[768,768]{1,0:T(8,128)(2,1)} %get-tuple-element.96.refs_0_.refs_4_, bf16[768,768]{1,0:T(8,128)(2,1)} %get-tuple-element.99.refs_1_.refs_3_.refs_5_, bf16[32,8,768]{2,1,0:T(8,128)(2,1)} %copy-done.8), custom_call_target="tpu_custom_call" | custom-call | tf_op jit(solution)/shard_map/pallas_call | solution.py:151
  94.4 6.8 %shard_map.198 = (f32[64,64]{1,0:T(8,128)}, f32[6,5,64,64]{3,2,1,0:T(8,128)}, f32[4,64,64]{2,1,0:T(8,128)}) custom-call(s32[1]{0:T(128)} %bitcast.refs_0_, bf16[128,768]{1,0:T(8,128)(2,1)} %get-tuple-element.102.refs_1_.refs_6_, bf16[128,768]{1,0:T(8,128)(2,1)} %get-tuple-element.103.refs_2_.refs_4_.refs_3_), custom_call_target="tpu_custom_call" | custom-call | tf_op jit(solution)/shard_map/pallas_call | solution.py:151
  101.3 12.7 %all-to-all-done.1.refs_0_ = bf16[32,40,128]{2,1,0:T(8,128)(2,1)S(1)} async-done(((bf16[32,40,128]{2,1,0:T(8,128)(2,1)}), bf16[32,40,128]{2,1,0:T(8,128)(2,1)S(1)}, u32[]{:S(2)}, u32[]{:S(2)}) %all-to-all-start.1) | async-done | bytes 327712 | tf_op jit(solution)/shard_map/all_to_all | solution.py:1095
  127.6 6.0 %shard_map.200 = (f32[768,768]{1,0:T(8,128)}, bf16[2,3,256,384]{3,2,1,0:T(8,128)(2,1)}) custom-call(bf16[768,768]{1,0:T(8,128)(2,1)} %get-tuple-element.106.refs_0_.refs_4_, bf16[768,768]{1,0:T(8,128)(2,1)} %get-tuple-element.99.refs_1_.refs_3_.refs_5_, bf16[2,16,768]{2,1,0:T(8,128)(2,1)} %copy-done.16, bf16[2,16,768]{2,1,0:T(8,128)(2,1)} %copy-done.15, ...), custom_call_target="tpu_custom_call" | custom-call | tf_op jit(solution)/shard_map/pallas_call | solution.py:151
  135.8 40.6 %shard_map.201 = (bf16[2,3,256,256]{3,2,1,0:T(8,128)(2,1)}, bf16[768,768]{1,0:T(8,128)(2,1)}, f32[768,768]{1,0:T(8,128)}, bf16[768,768]{1,0:T(8,128)(2,1)}, f32[...) custom-call(bf16[2,3,256,384]{3,2,1,0:T(8,128)(2,1)} %get-tuple-element.109.refs_0_.refs_1_, ...), custom_call_target="tpu_custom_call" | custom-call | tf_op jit(solution)/shard_map/pallas_call | solution.py:151
  176.4 6.7 %shard_map.202 = (f32[768,768]{1,0:T(8,128)}, f32[2,64,768]{2,1,0:T(8,128)}, bf16[32,32,128]{2,1,0:T(8,128)(2,1)}) custom-call(bf16[768,768]{1,0:T(8,128)(2,1)} %get-tuple-element.116.refs_0_, bf16[2,3,256,384]{3,2,1,0:T(8,128)(2,1)} %get-tuple-element.109.refs_0_.refs_1_, bf16[2,3,256,256]{3,2,1,0:T(8,128)(2,1)} %get-tuple-element.117.refs_2_, ...), custom_call_target="tpu_custom_call" | custom-call | tf_op jit(solution)/shard_map/pallas_call | solution.py:151
  183.1 9.0 %all-to-all-start.3 = ((bf16[32,32,128]{2,1,0:T(8,128)(2,1)}), bf16[32,32,128]{2,1,0:T(8,128)(2,1)S(1)}, u32[]{:S(2)}, u32[]{:S(2)}) async-start(bf16[32,32,128]{2,1,0:T(8,128)(2,1)} %get-tuple-element.118), calls=%async_computation.3 | async-start | bytes 524288 | tf_op jit(solution)/shard_map/all_to_all | solution.py:1095
  198.8 8.7 %shard_map.203 = (f32[768,768]{1,0:T(8,128)}, f32[3,4,256]{2,1,0:T(4,128)}) custom-call(bf16[768,768]{1,0:T(8,128)(2,1)} %get-tuple-element.116.refs_0_, bf16[2,16,768]{2,1,0:T(8,128)(2,1)} %copy-done.18, bf16[2,16,768]{2,1,0:T(8,128)(2,1)} %copy-done.17, bf16[768,768]{1,0:T(8,128)(2,1)} %get-tuple-element.99.refs_1_.refs_3_.refs_5_, ...), custom_call_target="tpu_custom_call" | custom-call | tf_op jit(solution)/shard_map/pallas_call | solution.py:151
  210.6 10.0 %all-to-all-start.4 = ((bf16[32,40,128]{2,1,0:T(8,128)(2,1)}), bf16[32,40,128]{2,1,0:T(8,128)(2,1)S(1)}, u32[]{:S(2)}, u32[]{:S(2)}) async-start(bf16[32,40,128]{2,1,0:T(8,128)(2,1)} %get-tuple-element.123), calls=%async_computation.4 | async-start | bytes 655360 | tf_op jit(solution)/shard_map/all_to_all | solution.py:1095
  220.6 8.7 %shard_map.205 = (f32[2,64,768]{2,1,0:T(8,128)}, f32[2,64,768]{2,1,0:T(8,128)}) custom-call(s32[1]{0:T(128)} %bitcast.refs_0_, f32[64,64]{1,0:T(8,128)} %get-tuple-element.125.refs_1_, f32[64,64]{1,0:T(8,128)} %get-tuple-element.104.refs_1_.refs_2_, f32[6,5,64,64]{3,2,1,0:T(8,128)} %get-tuple-element.126.refs_3_, f32[4,64,64]{2,1,0:T(8,128)} %get-tuple-element.127.refs_4_), custom_call_target="tpu_custom_call" | custom-call | tf_op jit(solution)/shard_map/pallas_call | solution.py:151
  233.4 8.8 %shard_map.206 = (f32[768,768]{1,0:T(8,128)}, f32[768,768]{1,0:T(8,128)}, bf16[32,8,768]{2,1,0:T(8,128)(2,1)}) custom-call(bf16[32,40,128]{2,1,0:T(8,128)(2,1)} %get-tuple-element.101.refs_0_, bf16[32,40,128]{2,1,0:T(8,128)(2,1)} %copy-done.7, bf16[32,40,128]{2,1,0:T(8,128)(2,1)} %copy-done.9, bf16[2,3,256,384]{3,2,1,0:T(8,128)(2,1)} %get-tuple-element.124.refs_3_, ...), custom_call_target="tpu_custom_call" | custom-call | tf_op jit(solution)/shard_map/pallas_call | solution.py:151
  246.7 14.9 %shard_map.207 = (f32[768,768]{1,0:T(8,128)}, f32[8,768]{1,0:T(8,128)}, f32[2,768,768]{2,1,0:T(8,128)}, bf16[16,24,768]{2,1,0:T(8,128)(2,1)}, bf16[16,24,768]{2,1,0:T(8,128)(2,1)}) custom-call(s32[1]{0:T(128)} %bitcast.refs_0_, bf16[768,768]{1,0:T(8,128)(2,1)} %bitcast.23, f32[768,768]{1,0:T(8,128)} %get-tuple-element.132.refs_2_, ...), custom_call_target="tpu_custom_call" | custom-call | tf_op jit(solution)/shard_map/pallas_call | solution.py:151
  261.6 6.0 %all-to-all-done.5.refs_1_.refs_0_ = bf16[32,8,768]{2,1,0:T(8,128)(2,1)S(1)} async-done(((bf16[32,8,768]{2,1,0:T(8,128)(2,1)}), bf16[32,8,768]{2,1,0:T(8,128)(2,1)S(1)}, u32[]{:S(2)}, u32[]{:S(2)}) %all-to-all-start.5) | async-done | bytes 393248 | tf_op jit(solution)/shard_map/all_to_all | solution.py:1095
  268.5 6.0 %shard_map.208 = (bf16[16,32,768]{2,1,0:T(8,128)(2,1)}, bf16[16,32,768]{2,1,0:T(8,128)(2,1)}, bf16[16,24,768]{2,1,0:T(8,128)(2,1)}, bf16[16,24,768]{2,1,0:T(8,128)(2,1)}) custom-call(s32[1]{0:T(128)} %bitcast.refs_0_, bf16[32,8,768]{2,1,0:T(8,128)(2,1)} %copy-done.6, f32[8,768]{1,0:T(8,128)} %get-tuple-element.139.refs_2_, ...), custom_call_target="tpu_custom_call" | custom-call | tf_op jit(solution)/shard_map/pallas_call | solution.py:151
  287.0 8.8 %collective-permute-done.16.refs_3_ = bf16[8,24,768]{2,1,0:T(8,128)(2,1)S(1)} collective-permute-done((bf16[8,24,768]{2,1,0:T(8,128)(2,1)}, bf16[8,24,768]{2,1,0:T(8,128)(2,1)S(1)}, u32[]{:S(2)}, u32[]{:S(2)}) %collective-permute-start.16) | collective-permute-done | bytes 294944 | tf_op jit(solution)/shard_map/ppermute | solution.py:190
  295.8 4.7 %collective-permute-done.17.refs_5_ = bf16[8,24,768]{2,1,0:T(8,128)(2,1)S(1)} collective-permute-done((bf16[8,24,768]{2,1,0:T(8,128)(2,1)}, bf16[8,24,768]{2,1,0:T(8,128)(2,1)S(1)}, u32[]{:S(2)}, u32[]{:S(2)}) %collective-permute-start.17) | collective-permute-done | bytes 294944 | tf_op jit(solution)/shard_map/ppermute | solution.py:190
  316.1 4.3 %collective-permute-done.22.refs_3_ = bf16[2,24,768]{2,1,0:T(8,128)(2,1)S(1)} collective-permute-done((bf16[2,24,768]{2,1,0:T(8,128)(2,1)S(1)}, bf16[2,24,768]{2,1,0:T(8,128)(2,1)S(1)}, u32[]{:S(2)}, u32[]{:S(2)}) %collective-permute-start.22) | collective-permute-done | bytes 73760 | tf_op jit(solution)/shard_map/ppermute | solution.py:190
  329.8 9.8 %reduce-scatter.2.cloned.1.call-done = bf16[1,9,24,768]{3,2,1,0:T(8,128)(2,1)} async-done(((bf16[32,9,24,768]{3,2,1,0:T(8,128)(2,1)}), bf16[1,9,24,768]{3,2,1,0:T(8,128)(2,1)}) %reduce-scatter.2.cloned.1.call-update) | async-done | bytes 331792 | tf_op jit(solution)/shard_map/reduce_scatter | solution.py:1285
  (128 shorter events, 108.2 us)
Async XLA Ops:
  7.2 127.9 %all-gather.3.cloned.1.call-start = ((), (), s32[]{:S(2)}) async-start(), calls=%async_computation.8 | async-start | bytes 10948608 | tf_op jit(solution)/shard_map/all_gather | solution.py:1135
  10.4 8.8 %collective-permute-start = (bf16[1,80,768]{2,1,0:T(8,128)(2,1)}, bf16[1,80,768]{2,1,0:T(8,128)(2,1)S(1)}, u32[]{:S(2)}, u32[]{:S(2)}) collective-permute-start(bf16[1,80,768]{2,1,0:T(8,128)(2,1)} %bitcast.28), channel_id=1, source_target_pairs={{0,24},{1,25},{2,26},{3,27},{4,28},{5,29},{6,30},{7,31},{8,16},{9,... | collective-permute-start | bytes 368648 | tf_op jit(solution)/shard_map/ppermute | solution.py:190
  20.0 7.6 %collective-permute-start.1 = (bf16[2,80,768]{2,1,0:T(8,128)(2,1)S(1)}, bf16[2,80,768]{2,1,0:T(8,128)(2,1)S(1)}, u32[]{:S(2)}, u32[]{:S(2)}) collective-permute-start(bf16[2,80,768]{2,1,0:T(8,128)(2,1)S(1)} %pad_maximum_fusion.5), channel_id=1, source_target_pairs={{0,8},{1,9},{2,10},{3,11},{4,12},{5,13},{6,14},{7,15},{8,0},{9,1},... | collective-permute-start | bytes 737288 | tf_op jit(solution)/shard_map/ppermute | solution.py:190
  28.7 6.4 %collective-permute-start.2 = (bf16[4,80,384]{2,1,0:T(8,128)(2,1)S(1)}, bf16[4,80,384]{2,1,0:T(8,128)(2,1)S(1)}, u32[]{:S(2)}, u32[]{:S(2)}) collective-permute-start(bf16[4,80,384]{2,1,0:T(8,128)(2,1)S(1)} %get-tuple-element.184), channel_id=1, source_target_pairs={{0,4},{1,5},{2,6},{3,7},{4,0},{5,1},{6,2},{7,3},{8,12},{9,13},{10,... | collective-permute-start | bytes 737288 | tf_op jit(solution)/shard_map/ppermute | solution.py:190
  30.2 7.2 %collective-permute-start.4 = (bf16[4,80,384]{2,1,0:T(8,128)(2,1)S(1)}, bf16[4,80,384]{2,1,0:T(8,128)(2,1)S(1)}, u32[]{:S(2)}, u32[]{:S(2)}) collective-permute-start(bf16[4,80,384]{2,1,0:T(8,128)(2,1)S(1)} %get-tuple-element.183), channel_id=1, source_target_pairs={{0,2},{1,3},{2,0},{3,1},{4,6},{5,7},{6,4},{7,5},{8,10},{9,11},{10,... | collective-permute-start | bytes 737288 | tf_op jit(solution)/shard_map/ppermute | solution.py:190
  35.2 14.2 %collective-permute-start.3 = (bf16[8,80,384]{2,1,0:T(8,128)(2,1)S(1)}, bf16[8,80,384]{2,1,0:T(8,128)(2,1)S(1)}, u32[]{:S(2)}, u32[]{:S(2)}) collective-permute-start(bf16[8,80,384]{2,1,0:T(8,128)(2,1)S(1)} %pad_maximum_fusion.3), channel_id=1, source_target_pairs={{0,2},{1,3},{2,0},{3,1},{4,6},{5,7},{6,4},{7,5},{8,10},{9,11},{10,... | collective-permute-start | bytes 1474568 | tf_op jit(solution)/shard_map/ppermute | solution.py:190
  37.5 12.2 %collective-permute-start.5 = (bf16[8,80,384]{2,1,0:T(8,128)(2,1)S(1)}, bf16[8,80,384]{2,1,0:T(8,128)(2,1)S(1)}, u32[]{:S(2)}, u32[]{:S(2)}) collective-permute-start(bf16[8,80,384]{2,1,0:T(8,128)(2,1)S(1)} %pad_maximum_fusion.4), channel_id=1, source_target_pairs={{0,4},{1,5},{2,6},{3,7},{4,0},{5,1},{6,2},{7,3},{8,12},{9,13},{10,... | collective-permute-start | bytes 1474568 | tf_op jit(solution)/shard_map/ppermute | solution.py:190
  59.8 23.6 %all-to-all-start = ((bf16[32,8,768]{2,1,0:T(8,128)(2,1)}), bf16[32,8,768]{2,1,0:T(8,128)(2,1)S(1)}, u32[]{:S(2)}, u32[]{:S(2)}) async-start(bf16[32,8,768]{2,1,0:T(8,128)(2,1)} %get-tuple-element.97), calls=%async_computation | async-start | bytes 786432 | tf_op jit(solution)/shard_map/all_to_all | solution.py:1095
  90.4 23.6 %all-to-all-start.1 = ((bf16[32,40,128]{2,1,0:T(8,128)(2,1)}), bf16[32,40,128]{2,1,0:T(8,128)(2,1)S(1)}, u32[]{:S(2)}, u32[]{:S(2)}) async-start(bf16[32,40,128]{2,1,0:T(8,128)(2,1)} %get-tuple-element.101.refs_0_), calls=%async_computation.1 | async-start | bytes 655360 | tf_op jit(solution)/shard_map/all_to_all | solution.py:1095
  117.3 17.8 %all-to-all-start.2 = ((bf16[32,40,128]{2,1,0:T(8,128)(2,1)}), bf16[32,40,128]{2,1,0:T(8,128)(2,1)S(1)}, u32[]{:S(2)}, u32[]{:S(2)}) async-start(bf16[32,40,128]{2,1,0:T(8,128)(2,1)} %get-tuple-element.105), calls=%async_computation.2 | async-start | bytes 655360 | tf_op jit(solution)/shard_map/all_to_all | solution.py:1095
  120.9 218.7 %reduce-scatter.2.cloned.1.call-start = ((), (), s32[]{:S(2)}) async-start(), calls=%async_computation.7 | async-start | bytes 10948608 | tf_op jit(solution)/shard_map/reduce_scatter | solution.py:1285
  183.1 24.3 %all-to-all-start.3 = ((bf16[32,32,128]{2,1,0:T(8,128)(2,1)}), bf16[32,32,128]{2,1,0:T(8,128)(2,1)S(1)}, u32[]{:S(2)}, u32[]{:S(2)}) async-start(bf16[32,32,128]{2,1,0:T(8,128)(2,1)} %get-tuple-element.118), calls=%async_computation.3 | async-start | bytes 524288 | tf_op jit(solution)/shard_map/all_to_all | solution.py:1095
  210.6 22.0 %all-to-all-start.4 = ((bf16[32,40,128]{2,1,0:T(8,128)(2,1)}), bf16[32,40,128]{2,1,0:T(8,128)(2,1)S(1)}, u32[]{:S(2)}, u32[]{:S(2)}) async-start(bf16[32,40,128]{2,1,0:T(8,128)(2,1)} %get-tuple-element.123), calls=%async_computation.4 | async-start | bytes 655360 | tf_op jit(solution)/shard_map/all_to_all | solution.py:1095
  242.1 25.5 %all-to-all-start.5 = ((bf16[32,8,768]{2,1,0:T(8,128)(2,1)}), bf16[32,8,768]{2,1,0:T(8,128)(2,1)S(1)}, u32[]{:S(2)}, u32[]{:S(2)}) async-start(bf16[32,8,768]{2,1,0:T(8,128)(2,1)} %get-tuple-element.131), calls=%async_computation.5 | async-start | bytes 786432 | tf_op jit(solution)/shard_map/all_to_all | solution.py:1095
  283.9 16.7 %collective-permute-start.15 = (bf16[8,32,768]{2,1,0:T(8,128)(2,1)}, bf16[8,32,768]{2,1,0:T(8,128)(2,1)S(1)}, u32[]{:S(2)}, u32[]{:S(2)}) collective-permute-start(bf16[8,32,768]{2,1,0:T(8,128)(2,1)} %get-tuple-element.152), channel_id=1, source_target_pairs={{0,2},{1,3},{2,0},{3,1},{4,6},{5,7},{6,4},{7,5},{8,10},{9,11},{10,... | collective-permute-start | bytes 1179656 | tf_op jit(solution)/shard_map/ppermute | solution.py:190
  285.5 10.4 %collective-permute-start.16 = (bf16[8,24,768]{2,1,0:T(8,128)(2,1)}, bf16[8,24,768]{2,1,0:T(8,128)(2,1)S(1)}, u32[]{:S(2)}, u32[]{:S(2)}) collective-permute-start(bf16[8,24,768]{2,1,0:T(8,128)(2,1)} %get-tuple-element.154), channel_id=1, source_target_pairs={{0,4},{1,5},{2,6},{3,7},{4,0},{5,1},{6,2},{7,3},{8,12},{9,13},{10,... | collective-permute-start | bytes 884744 | tf_op jit(solution)/shard_map/ppermute | solution.py:190
  287.0 13.6 %collective-permute-start.17 = (bf16[8,24,768]{2,1,0:T(8,128)(2,1)}, bf16[8,24,768]{2,1,0:T(8,128)(2,1)S(1)}, u32[]{:S(2)}, u32[]{:S(2)}) collective-permute-start(bf16[8,24,768]{2,1,0:T(8,128)(2,1)} %get-tuple-element.156), channel_id=1, source_target_pairs={{0,8},{1,9},{2,10},{3,11},{4,12},{5,13},{6,14},{7,15},{8,0},{9,1},... | collective-permute-start | bytes 884744 | tf_op jit(solution)/shard_map/ppermute | solution.py:190
  304.1 8.9 %collective-permute-start.18 = (bf16[4,32,768]{2,1,0:T(8,128)(2,1)S(1)}, bf16[4,32,768]{2,1,0:T(8,128)(2,1)S(1)}, u32[]{:S(2)}, u32[]{:S(2)}) collective-permute-start(bf16[4,32,768]{2,1,0:T(8,128)(2,1)S(1)} %get-tuple-element.158), channel_id=1, source_target_pairs={{0,4},{1,5},{2,6},{3,7},{4,0},{5,1},{6,2},{7,3},{8,12},{9,13},{10,... | collective-permute-start | bytes 589832 | tf_op jit(solution)/shard_map/ppermute | solution.py:190
  304.1 5.2 %collective-permute-start.19 = (bf16[4,24,768]{2,1,0:T(8,128)(2,1)S(1)}, bf16[4,24,768]{2,1,0:T(8,128)(2,1)S(1)}, u32[]{:S(2)}, u32[]{:S(2)}) collective-permute-start(bf16[4,24,768]{2,1,0:T(8,128)(2,1)S(1)} %get-tuple-element.160), channel_id=1, source_target_pairs={{0,2},{1,3},{2,0},{3,1},{4,6},{5,7},{6,4},{7,5},{8,10},{9,11},{10,... | collective-permute-start | bytes 442376 | tf_op jit(solution)/shard_map/ppermute | solution.py:190
  304.5 8.4 %collective-permute-start.20 = (bf16[4,24,768]{2,1,0:T(8,128)(2,1)S(1)}, bf16[4,24,768]{2,1,0:T(8,128)(2,1)S(1)}, u32[]{:S(2)}, u32[]{:S(2)}) collective-permute-start(bf16[4,24,768]{2,1,0:T(8,128)(2,1)S(1)} %get-tuple-element.162), channel_id=1, source_target_pairs={{0,24},{1,25},{2,26},{3,27},{4,28},{5,29},{6,30},{7,31},{8,16},{9,... | collective-permute-start | bytes 442376 | tf_op jit(solution)/shard_map/ppermute | solution.py:190
  313.0 7.4 %collective-permute-start.21 = (bf16[2,56,768]{2,1,0:T(8,128)(2,1)S(1)}, bf16[2,56,768]{2,1,0:T(8,128)(2,1)S(1)}, u32[]{:S(2)}, u32[]{:S(2)}) collective-permute-start(bf16[2,56,768]{2,1,0:T(8,128)(2,1)S(1)} %get-tuple-element.164), channel_id=1, source_target_pairs={{0,8},{1,9},{2,10},{3,11},{4,12},{5,13},{6,14},{7,15},{8,0},{9,1},... | collective-permute-start | bytes 516104 | tf_op jit(solution)/shard_map/ppermute | solution.py:190
  316.1 4.4 %collective-permute-start.22 = (bf16[2,24,768]{2,1,0:T(8,128)(2,1)S(1)}, bf16[2,24,768]{2,1,0:T(8,128)(2,1)S(1)}, u32[]{:S(2)}, u32[]{:S(2)}) collective-permute-start(bf16[2,24,768]{2,1,0:T(8,128)(2,1)S(1)} %get-tuple-element.166), channel_id=1, source_target_pairs={{0,2},{1,3},{2,0},{3,1},{4,6},{5,7},{6,4},{7,5},{8,10},{9,11},{10,... | collective-permute-start | bytes 221192 | tf_op jit(solution)/shard_map/ppermute | solution.py:190
  320.5 7.3 %collective-permute-start.23 = (bf16[1,56,768]{2,1,0:T(8,128)(2,1)S(1)}, bf16[1,56,768]{2,1,0:T(8,128)(2,1)S(1)}, u32[]{:S(2)}, u32[]{:S(2)}) collective-permute-start(bf16[1,56,768]{2,1,0:T(8,128)(2,1)S(1)} %get-tuple-element.168), channel_id=1, source_target_pairs={{0,24},{1,25},{2,26},{3,27},{4,28},{5,29},{6,30},{7,31},{8,16},{9,... | collective-permute-start | bytes 258056 | tf_op jit(solution)/shard_map/ppermute | solution.py:190
  322.9 4.9 %collective-permute-start.24 = (bf16[1,24,768]{2,1,0:T(8,128)(2,1)S(1)}, bf16[1,24,768]{2,1,0:T(8,128)(2,1)S(1)}, u32[]{:S(2)}, u32[]{:S(2)}) collective-permute-start(bf16[1,24,768]{2,1,0:T(8,128)(2,1)S(1)} %get-tuple-element.170), channel_id=1, source_target_pairs={{0,4},{1,5},{2,6},{3,7},{4,0},{5,1},{6,2},{7,3},{8,12},{9,13},{10,... | collective-permute-start | bytes 110600 | tf_op jit(solution)/shard_map/ppermute | solution.py:190
  (29 other events, 63.7 us)
Sparse Core Ops, SparseCore 0:
  28.7 105.0 all-gather.2
  176.6 163.0 reduce-scatter.1
where the time goes:
time: 350 us; the launch traced here: 348 us
  Pallas kernels  146 us (42%)
  waiting for transfers between devices  102 us (29%)
  starting transfers between devices  67.3 us (19%)
  local copies, waits for them, and re-layouts  15 us (4%)
  between operations  14.5 us (4%)
  other arithmetic  3.52 us (1%)
    pallas_call x18, Pallas kernels, vmem_call(): pl.pallas_call(run, out_shape=outs, in_specs=[pl.BlockSpec(memory_space=p...  145 us
    ppermute x21, waiting for transfers between devices, swap(): return lax.ppermute(x, AX, [(i, i ^ mask) for i in range(n)])  56.2 us
    all_to_all x6, waiting for transfers between devices, exchange(): return lax.all_to_all(x, AX, 0, 0, tiled=True)  34.6 us
    all_to_all x6, starting transfers between devices, exchange(): return lax.all_to_all(x, AX, 0, 0, tiled=True)  33.4 us
    ppermute x21, starting transfers between devices, swap(): return lax.ppermute(x, AX, [(i, i ^ mask) for i in range(n)])  25.2 us
    reduce_scatter x1, waiting for transfers between devices, per_device(): early = lax.psum_scatter(grads[0], AX, scatter_dimension=0, tiled=False)  9.79 us
    unnamed x40, local copies, waits for them, and re-layouts  9.3 us
  transfers between devices with their start and end apart: 33, of which 23 were waited for; matrix products, arithmetic and copies ran while one was open for 2% of the time, Pallas kernels for 29%

commit v1 on v0

--- a/solution.py
+++ b/solution.py
@@ -209,10 +209,11 @@
 def cube_gather(piece, n, core):
     buf = piece[None]
     first, second = gather_order(n, core, 0), gather_order(n, core, 1)
+    mid = None
     for dim in first[:-2]:
         buf = jnp.concatenate([buf, swap(buf, n, dim)], axis=0)
+        mid = buf if mid is None else mid
     half = piece.shape[1] // 2
-    mid = buf
     bufs = [buf[:, :, :half], buf[:, :, half:]]
     for dims in zip(first[-2:], second[-2:]):
         got = [swap(x, n, dim) for x, dim in zip(bufs, dims)]
@@ -1210,11 +1211,12 @@
         (me, q_land, k_land),
         scalars=1,
     )
+    v_low, v_high = halo(values)
+    got_sums, v_low, v_high = lax.optimization_barrier((got_sums, v_low, v_high))
     stat, summary = vmem_call(
         combine_kernel, (slots, shape_of((M, 128), f32)), (got_sums, inverse)
     )
     stat = exchange(stat)
-    v_low, v_high = halo(values)
     convolved, k1 = vmem_call(
         kernel1_kernel,
         (square_full, shape_of((2, groups, GW, held), bf16)),

time: 350 us -> 336 us (0.960)
  starting transfers between devices: 67.3 us -> 56.5 us
    ppermute x21, waiting for transfers between devices: 56.2 us -> 65.3 us  [swap(): return lax.ppermute(x, AX, [(i, i ^ mask) for i in range(n)])]
    all_to_all x6, starting transfers between devices: 33.4 us -> 27.2 us  [exchange(): return lax.all_to_all(x, AX, 0, 0, tiled=True)]
    all_to_all x6, waiting for transfers between devices: 34.6 us -> 28.6 us  [exchange(): return lax.all_to_all(x, AX, 0, 0, tiled=True)]
    ppermute x21, starting transfers between devices: 25.2 us -> 20.6 us  [swap(): return lax.ppermute(x, AX, [(i, i ^ mask) for i in range(n)])]
    reduce_scatter x1, waiting for transfers between devices: 9.79 us -> 5.43 us  [per_device(): early = lax.psum_scatter(grads[0], AX, scatter_dimension=0, tiled=False)]
  transfers between devices with their start and end apart: 33 -> 33, of which waited for: 23 -> 24; matrix products, arithmetic and copies ran while one was open for 2% -> 2% of each run, Pallas kernels for 29% -> 30%
where the time goes in v1:
time: 336 us; the launch traced here: 335 us
  Pallas kernels  146 us (43%)
  waiting for transfers between devices  100 us (30%)
  starting transfers between devices  56.5 us (17%)
  between operations  14.5 us (4%)
  local copies, waits for them, and re-layouts  14.4 us (4%)
  other arithmetic  3.51 us (1%)
    pallas_call x18, Pallas kernels, vmem_call(): pl.pallas_call(run, out_shape=outs, in_specs=[pl.BlockSpec(memory_space=p...  145 us
    ppermute x21, waiting for transfers between devices, swap(): return lax.ppermute(x, AX, [(i, i ^ mask) for i in range(n)])  65.3 us
    all_to_all x6, waiting for transfers between devices, exchange(): return lax.all_to_all(x, AX, 0, 0, tiled=True)  28.6 us
    all_to_all x6, starting transfers between devices, exchange(): return lax.all_to_all(x, AX, 0, 0, tiled=True)  27.2 us
    ppermute x21, starting transfers between devices, swap(): return lax.ppermute(x, AX, [(i, i ^ mask) for i in range(n)])  20.6 us
    unnamed x40, local copies, waits for them, and re-layouts  8.69 us
  transfers between devices with their start and end apart: 33, of which 24 were waited for; matrix products, arithmetic and copies ran while one was open for 2% of the time, Pallas kernels for 30%

profile of v1, /device:TPU:0, one launch (start us, length us, event | category | flops | bytes accessed | tf_op | source)
XLA Modules:
  0.0 335.2 jit_solution(1921498962306632871)
XLA Ops:
  31.7 5.7 %collective-permute-done.2 = bf16[4,80,384]{2,1,0:T(8,128)(2,1)S(1)} collective-permute-done((bf16[4,80,384]{2,1,0:T(8,128)(2,1)S(1)}, bf16[4,80,384]{2,1,0:T(8,128)(2,1)S(1)}, u32[]{:S(2)}, u32[]{:S(2)}) %collective-permute-start.2) | collective-permute-done | bytes 245792 | tf_op jit(solution)/shard_map/ppermute | solution.py:190
  40.7 8.5 %collective-permute-done.3 = bf16[8,80,384]{2,1,0:T(8,128)(2,1)S(1)} collective-permute-done((bf16[8,80,384]{2,1,0:T(8,128)(2,1)S(1)}, bf16[8,80,384]{2,1,0:T(8,128)(2,1)S(1)}, u32[]{:S(2)}, u32[]{:S(2)}) %collective-permute-start.3) | collective-permute-done | bytes 491552 | tf_op jit(solution)/shard_map/ppermute | solution.py:190
  53.6 6.1 %shard_map.195 = (bf16[768,768]{1,0:T(8,128)(2,1)}, bf16[768,768]{1,0:T(8,128)(2,1)}, bf16[32,8,768]{2,1,0:T(8,128)(2,1)}, bf16[2,768,768]{2,1,0:T(8,128)(2,1)}) custom-call(s32[1]{0:T(128)} %bitcast.refs_0_, bf16[768,768]{1,0:T(8,128)(2,1)} %bitcast.20, bf16[16,80,384]{2,1,0:T(8,128)(2,1)} %copy-done.3, bf16[16,80,384]{2,1,0:T(8,128)(2,1)} %copy-done.4, ...), custom_call_target="tpu_custom_call" | custom-call | tf_op jit(solution)/shard_map/pallas_call | solution.py:151
  63.3 8.4 %shard_map.196 = (bf16[768,768]{1,0:T(8,128)(2,1)}, bf16[12,128,160]{2,1,0:T(8,128)(2,1)}, bf16[12,128,160]{2,1,0:T(8,128)(2,1)}, f32[8,768]{1,0:T(8,128)}, bf16[768,768]{1,0:T(8,128)(2,1)}) custom-call(s32[1]{0:T(128)} %bitcast.refs_0_, bf16[768,768]{1,0:T(8,128)(2,1)} %bitcast.21, bf16[16,80,384]{2,1,0:T(8,128)(2,1)} %copy-done.3, ...), custom_call_target="tpu_custom_call" | custom-call | tf_op jit(solution)/shard_map/pallas_call | solution.py:151
  71.7 6.6 %all-to-all-done.refs_2_ = bf16[32,8,768]{2,1,0:T(8,128)(2,1)S(1)} async-done(((bf16[32,8,768]{2,1,0:T(8,128)(2,1)}), bf16[32,8,768]{2,1,0:T(8,128)(2,1)S(1)}, u32[]{:S(2)}, u32[]{:S(2)}) %all-to-all-start) | async-done | bytes 393248 | tf_op jit(solution)/shard_map/all_to_all | solution.py:1096
  79.0 6.7 %shard_map.197 = (bf16[128,768]{1,0:T(8,128)(2,1)}, bf16[128,768]{1,0:T(8,128)(2,1)}, bf16[2,3,256,384]{3,2,1,0:T(8,128)(2,1)}, bf16[32,40,128]{2,1,0:T(8,128)(2,1)}) custom-call(bf16[768,768]{1,0:T(8,128)(2,1)} %get-tuple-element.99.refs_0_.refs_4_, bf16[768,768]{1,0:T(8,128)(2,1)} %get-tuple-element.102.refs_1_.refs_3_.refs_5_, bf16[32,8,768]{2,1,0:T(8,128)(2,1)} %copy-done.8), custom_call_target="tpu_custom_call" | custom-call | tf_op jit(solution)/shard_map/pallas_call | solution.py:151
  93.7 6.8 %shard_map.198 = (f32[64,64]{1,0:T(8,128)}, f32[6,5,64,64]{3,2,1,0:T(8,128)}, f32[4,64,64]{2,1,0:T(8,128)}) custom-call(s32[1]{0:T(128)} %bitcast.refs_0_, bf16[128,768]{1,0:T(8,128)(2,1)} %get-tuple-element.106.refs_1_.refs_6_, bf16[128,768]{1,0:T(8,128)(2,1)} %get-tuple-element.107.refs_2_.refs_4_.refs_3_), custom_call_target="tpu_custom_call" | custom-call | tf_op jit(solution)/shard_map/pallas_call | solution.py:151
  100.5 6.9 %all-to-all-done.1.refs_0_ = bf16[32,40,128]{2,1,0:T(8,128)(2,1)S(1)} async-done(((bf16[32,40,128]{2,1,0:T(8,128)(2,1)}), bf16[32,40,128]{2,1,0:T(8,128)(2,1)S(1)}, u32[]{:S(2)}, u32[]{:S(2)}) %all-to-all-start.1) | async-done | bytes 327712 | tf_op jit(solution)/shard_map/all_to_all | solution.py:1096
  110.8 5.4 %all-to-all-start.2 = ((bf16[32,40,128]{2,1,0:T(8,128)(2,1)}), bf16[32,40,128]{2,1,0:T(8,128)(2,1)S(1)}, u32[]{:S(2)}, u32[]{:S(2)}) async-start(bf16[32,40,128]{2,1,0:T(8,128)(2,1)} %get-tuple-element.109), calls=%async_computation.2 | async-start | bytes 655360 | tf_op jit(solution)/shard_map/all_to_all | solution.py:1096
  116.3 6.1 %shard_map.200 = (f32[768,768]{1,0:T(8,128)}, bf16[2,3,256,384]{3,2,1,0:T(8,128)(2,1)}) custom-call(bf16[768,768]{1,0:T(8,128)(2,1)} %get-tuple-element.110.refs_0_.refs_4_, bf16[768,768]{1,0:T(8,128)(2,1)} %get-tuple-element.102.refs_1_.refs_3_.refs_5_, bf16[2,16,768]{2,1,0:T(8,128)(2,1)} %copy-done.16, bf16[2,16,768]{2,1,0:T(8,128)(2,1)} %copy-done.15, ...), custom_call_target="tpu_custom_call" | custom-call | tf_op jit(solution)/shard_map/pallas_call | solution.py:151
  122.4 5.8 %all-to-all-done.2.refs_2_.refs_1_ = bf16[32,40,128]{2,1,0:T(8,128)(2,1)S(1)} async-done(((bf16[32,40,128]{2,1,0:T(8,128)(2,1)}), bf16[32,40,128]{2,1,0:T(8,128)(2,1)S(1)}, u32[]{:S(2)}, u32[]{:S(2)}) %all-to-all-start.2) | async-done | bytes 327712 | tf_op jit(solution)/shard_map/all_to_all | solution.py:1096
  128.9 40.6 %shard_map.201 = (bf16[2,3,256,256]{3,2,1,0:T(8,128)(2,1)}, bf16[768,768]{1,0:T(8,128)(2,1)}, f32[768,768]{1,0:T(8,128)}, bf16[768,768]{1,0:T(8,128)(2,1)}, f32[...) custom-call(bf16[2,3,256,384]{3,2,1,0:T(8,128)(2,1)} %get-tuple-element.115.refs_0_.refs_1_, ...), custom_call_target="tpu_custom_call" | custom-call | tf_op jit(solution)/shard_map/pallas_call | solution.py:151
  169.5 6.7 %shard_map.202 = (f32[768,768]{1,0:T(8,128)}, f32[2,64,768]{2,1,0:T(8,128)}, bf16[32,32,128]{2,1,0:T(8,128)(2,1)}) custom-call(bf16[768,768]{1,0:T(8,128)(2,1)} %get-tuple-element.122.refs_0_, bf16[2,3,256,384]{3,2,1,0:T(8,128)(2,1)} %get-tuple-element.115.refs_0_.refs_1_, bf16[2,3,256,256]{3,2,1,0:T(8,128)(2,1)} %get-tuple-element.123.refs_2_, ...), custom_call_target="tpu_custom_call" | custom-call | tf_op jit(solution)/shard_map/pallas_call | solution.py:151
  185.7 8.7 %shard_map.203 = (f32[768,768]{1,0:T(8,128)}, f32[3,4,256]{2,1,0:T(4,128)}) custom-call(bf16[768,768]{1,0:T(8,128)(2,1)} %get-tuple-element.122.refs_0_, bf16[2,16,768]{2,1,0:T(8,128)(2,1)} %copy-done.18, bf16[2,16,768]{2,1,0:T(8,128)(2,1)} %copy-done.17, bf16[768,768]{1,0:T(8,128)(2,1)} %get-tuple-element.102.refs_1_.refs_3_.refs_5_, ...), custom_call_target="tpu_custom_call" | custom-call | tf_op jit(solution)/shard_map/pallas_call | solution.py:151
  197.6 10.0 %all-to-all-start.4 = ((bf16[32,40,128]{2,1,0:T(8,128)(2,1)}), bf16[32,40,128]{2,1,0:T(8,128)(2,1)S(1)}, u32[]{:S(2)}, u32[]{:S(2)}) async-start(bf16[32,40,128]{2,1,0:T(8,128)(2,1)} %get-tuple-element.129), calls=%async_computation.4 | async-start | bytes 655360 | tf_op jit(solution)/shard_map/all_to_all | solution.py:1096
  207.6 8.7 %shard_map.205 = (f32[2,64,768]{2,1,0:T(8,128)}, f32[2,64,768]{2,1,0:T(8,128)}) custom-call(s32[1]{0:T(128)} %bitcast.refs_0_, f32[64,64]{1,0:T(8,128)} %get-tuple-element.131.refs_1_, f32[64,64]{1,0:T(8,128)} %get-tuple-element.108.refs_1_.refs_2_, f32[6,5,64,64]{3,2,1,0:T(8,128)} %get-tuple-element.132.refs_3_, f32[4,64,64]{2,1,0:T(8,128)} %get-tuple-element.133.refs_4_), custom_call_target="tpu_custom_call" | custom-call | tf_op jit(solution)/shard_map/pallas_call | solution.py:151
  220.3 8.5 %shard_map.206 = (f32[768,768]{1,0:T(8,128)}, f32[768,768]{1,0:T(8,128)}, bf16[32,8,768]{2,1,0:T(8,128)(2,1)}) custom-call(bf16[32,40,128]{2,1,0:T(8,128)(2,1)} %get-tuple-element.104.refs_0_, bf16[32,40,128]{2,1,0:T(8,128)(2,1)} %copy-done.7, bf16[32,40,128]{2,1,0:T(8,128)(2,1)} %copy-done.9, bf16[2,3,256,384]{3,2,1,0:T(8,128)(2,1)} %get-tuple-element.130.refs_3_, ...), custom_call_target="tpu_custom_call" | custom-call | tf_op jit(solution)/shard_map/pallas_call | solution.py:151
  233.5 14.9 %shard_map.207 = (f32[768,768]{1,0:T(8,128)}, f32[8,768]{1,0:T(8,128)}, f32[2,768,768]{2,1,0:T(8,128)}, bf16[16,24,768]{2,1,0:T(8,128)(2,1)}, bf16[16,24,768]{2,1,0:T(8,128)(2,1)}) custom-call(s32[1]{0:T(128)} %bitcast.refs_0_, bf16[768,768]{1,0:T(8,128)(2,1)} %bitcast.23, f32[768,768]{1,0:T(8,128)} %get-tuple-element.138.refs_2_, ...), custom_call_target="tpu_custom_call" | custom-call | tf_op jit(solution)/shard_map/pallas_call | solution.py:151
  248.4 6.1 %all-to-all-done.5.refs_1_.refs_0_ = bf16[32,8,768]{2,1,0:T(8,128)(2,1)S(1)} async-done(((bf16[32,8,768]{2,1,0:T(8,128)(2,1)}), bf16[32,8,768]{2,1,0:T(8,128)(2,1)S(1)}, u32[]{:S(2)}, u32[]{:S(2)}) %all-to-all-start.5) | async-done | bytes 393248 | tf_op jit(solution)/shard_map/all_to_all | solution.py:1096
  255.2 6.1 %shard_map.208 = (bf16[16,32,768]{2,1,0:T(8,128)(2,1)}, bf16[16,32,768]{2,1,0:T(8,128)(2,1)}, bf16[16,24,768]{2,1,0:T(8,128)(2,1)}, bf16[16,24,768]{2,1,0:T(8,128)(2,1)}) custom-call(s32[1]{0:T(128)} %bitcast.refs_0_, bf16[32,8,768]{2,1,0:T(8,128)(2,1)} %copy-done.6, f32[8,768]{1,0:T(8,128)} %get-tuple-element.145.refs_2_, ...), custom_call_target="tpu_custom_call" | custom-call | tf_op jit(solution)/shard_map/pallas_call | solution.py:151
  274.7 9.9 %collective-permute-done.16.refs_3_ = bf16[8,24,768]{2,1,0:T(8,128)(2,1)S(1)} collective-permute-done((bf16[8,24,768]{2,1,0:T(8,128)(2,1)}, bf16[8,24,768]{2,1,0:T(8,128)(2,1)S(1)}, u32[]{:S(2)}, u32[]{:S(2)}) %collective-permute-start.16) | collective-permute-done | bytes 294944 | tf_op jit(solution)/shard_map/ppermute | solution.py:190
  284.7 5.4 %collective-permute-done.17.refs_5_ = bf16[8,24,768]{2,1,0:T(8,128)(2,1)S(1)} collective-permute-done((bf16[8,24,768]{2,1,0:T(8,128)(2,1)}, bf16[8,24,768]{2,1,0:T(8,128)(2,1)S(1)}, u32[]{:S(2)}, u32[]{:S(2)}) %collective-permute-start.17) | collective-permute-done | bytes 294944 | tf_op jit(solution)/shard_map/ppermute | solution.py:190
  298.8 6.5 %collective-permute-done.20.refs_5_ = bf16[4,24,768]{2,1,0:T(8,128)(2,1)S(1)} collective-permute-done((bf16[4,24,768]{2,1,0:T(8,128)(2,1)S(1)}, bf16[4,24,768]{2,1,0:T(8,128)(2,1)S(1)}, u32[]{:S(2)}, u32[]{:S(2)}) %collective-permute-start.20) | collective-permute-done | bytes 147488 | tf_op jit(solution)/shard_map/ppermute | solution.py:190
  321.1 5.4 %reduce-scatter.2.cloned.1.call-done = bf16[1,9,24,768]{3,2,1,0:T(8,128)(2,1)} async-done(((bf16[32,9,24,768]{3,2,1,0:T(8,128)(2,1)}), bf16[1,9,24,768]{3,2,1,0:T(8,128)(2,1)}) %reduce-scatter.2.cloned.1.call-update) | async-done | bytes 331792 | tf_op jit(solution)/shard_map/reduce_scatter | solution.py:1287
  (128 shorter events, 110.2 us)
Async XLA Ops:
  7.2 121.0 %all-gather.3.cloned.1.call-start = ((), (), s32[]{:S(2)}) async-start(), calls=%async_computation.8 | async-start | bytes 10948608 | tf_op jit(solution)/shard_map/all_gather | solution.py:1136
  10.4 8.8 %collective-permute-start = (bf16[1,80,768]{2,1,0:T(8,128)(2,1)}, bf16[1,80,768]{2,1,0:T(8,128)(2,1)S(1)}, u32[]{:S(2)}, u32[]{:S(2)}) collective-permute-start(bf16[1,80,768]{2,1,0:T(8,128)(2,1)} %bitcast.28), channel_id=1, source_target_pairs={{0,24},{1,25},{2,26},{3,27},{4,28},{5,29},{6,30},{7,31},{8,16},{9,... | collective-permute-start | bytes 368648 | tf_op jit(solution)/shard_map/ppermute | solution.py:190
  20.1 7.6 %collective-permute-start.1 = (bf16[2,80,768]{2,1,0:T(8,128)(2,1)S(1)}, bf16[2,80,768]{2,1,0:T(8,128)(2,1)S(1)}, u32[]{:S(2)}, u32[]{:S(2)}) collective-permute-start(bf16[2,80,768]{2,1,0:T(8,128)(2,1)S(1)} %pad_maximum_fusion.5), channel_id=1, source_target_pairs={{0,8},{1,9},{2,10},{3,11},{4,12},{5,13},{6,14},{7,15},{8,0},{9,1},... | collective-permute-start | bytes 737288 | tf_op jit(solution)/shard_map/ppermute | solution.py:190
  28.7 8.8 %collective-permute-start.2 = (bf16[4,80,384]{2,1,0:T(8,128)(2,1)S(1)}, bf16[4,80,384]{2,1,0:T(8,128)(2,1)S(1)}, u32[]{:S(2)}, u32[]{:S(2)}) collective-permute-start(bf16[4,80,384]{2,1,0:T(8,128)(2,1)S(1)} %get-tuple-element.190), channel_id=1, source_target_pairs={{0,4},{1,5},{2,6},{3,7},{4,0},{5,1},{6,2},{7,3},{8,12},{9,13},{10,... | collective-permute-start | bytes 737288 | tf_op jit(solution)/shard_map/ppermute | solution.py:190
  30.2 10.2 %collective-permute-start.4 = (bf16[4,80,384]{2,1,0:T(8,128)(2,1)S(1)}, bf16[4,80,384]{2,1,0:T(8,128)(2,1)S(1)}, u32[]{:S(2)}, u32[]{:S(2)}) collective-permute-start(bf16[4,80,384]{2,1,0:T(8,128)(2,1)S(1)} %get-tuple-element.189), channel_id=1, source_target_pairs={{0,2},{1,3},{2,0},{3,1},{4,6},{5,7},{6,4},{7,5},{8,10},{9,11},{10,... | collective-permute-start | bytes 737288 | tf_op jit(solution)/shard_map/ppermute | solution.py:190
  37.5 11.7 %collective-permute-start.3 = (bf16[8,80,384]{2,1,0:T(8,128)(2,1)S(1)}, bf16[8,80,384]{2,1,0:T(8,128)(2,1)S(1)}, u32[]{:S(2)}, u32[]{:S(2)}) collective-permute-start(bf16[8,80,384]{2,1,0:T(8,128)(2,1)S(1)} %pad_maximum_fusion.3), channel_id=1, source_target_pairs={{0,2},{1,3},{2,0},{3,1},{4,6},{5,7},{6,4},{7,5},{8,10},{9,11},{10,... | collective-permute-start | bytes 1474568 | tf_op jit(solution)/shard_map/ppermute | solution.py:190
  40.5 9.4 %collective-permute-start.5 = (bf16[8,80,384]{2,1,0:T(8,128)(2,1)S(1)}, bf16[8,80,384]{2,1,0:T(8,128)(2,1)S(1)}, u32[]{:S(2)}, u32[]{:S(2)}) collective-permute-start(bf16[8,80,384]{2,1,0:T(8,128)(2,1)S(1)} %pad_maximum_fusion.4), channel_id=1, source_target_pairs={{0,4},{1,5},{2,6},{3,7},{4,0},{5,1},{6,2},{7,3},{8,12},{9,13},{10,... | collective-permute-start | bytes 1474568 | tf_op jit(solution)/shard_map/ppermute | solution.py:190
  59.7 18.6 %all-to-all-start = ((bf16[32,8,768]{2,1,0:T(8,128)(2,1)}), bf16[32,8,768]{2,1,0:T(8,128)(2,1)S(1)}, u32[]{:S(2)}, u32[]{:S(2)}) async-start(bf16[32,8,768]{2,1,0:T(8,128)(2,1)} %get-tuple-element.100), calls=%async_computation | async-start | bytes 786432 | tf_op jit(solution)/shard_map/all_to_all | solution.py:1096
  85.7 21.8 %all-to-all-start.1 = ((bf16[32,40,128]{2,1,0:T(8,128)(2,1)}), bf16[32,40,128]{2,1,0:T(8,128)(2,1)S(1)}, u32[]{:S(2)}, u32[]{:S(2)}) async-start(bf16[32,40,128]{2,1,0:T(8,128)(2,1)} %get-tuple-element.104.refs_0_), calls=%async_computation.1 | async-start | bytes 655360 | tf_op jit(solution)/shard_map/all_to_all | solution.py:1096
  89.3 11.2 %collective-permute-start.9 = (bf16[2,16,768]{2,1,0:T(8,128)(2,1)S(1)}, bf16[2,16,768]{2,1,0:T(8,128)(2,1)S(1)}, u32[]{:S(2)}, u32[]{:S(2)}) collective-permute-start(bf16[2,16,768]{2,1,0:T(8,128)(2,1)S(1)} %get-tuple-element.187), channel_id=1, source_target_pairs={{1,0},{2,1},{3,2},{4,3},{5,4},{6,5},{7,6},{8,7},{9,8},{10,9},{11,1... | collective-permute-start | bytes 147464 | tf_op jit(solution)/shard_map/ppermute | solution.py:1194
  90.6 9.9 %collective-permute-start.8 = (bf16[2,16,768]{2,1,0:T(8,128)(2,1)S(1)}, bf16[2,16,768]{2,1,0:T(8,128)(2,1)S(1)}, u32[]{:S(2)}, u32[]{:S(2)}) collective-permute-start(bf16[2,16,768]{2,1,0:T(8,128)(2,1)S(1)} %get-tuple-element.188), channel_id=1, source_target_pairs={{0,1},{1,2},{2,3},{3,4},{4,5},{5,6},{6,7},{7,8},{8,9},{9,10},{10,1... | collective-permute-start | bytes 147464 | tf_op jit(solution)/shard_map/ppermute | solution.py:1193
  110.8 17.4 %all-to-all-start.2 = ((bf16[32,40,128]{2,1,0:T(8,128)(2,1)}), bf16[32,40,128]{2,1,0:T(8,128)(2,1)S(1)}, u32[]{:S(2)}, u32[]{:S(2)}) async-start(bf16[32,40,128]{2,1,0:T(8,128)(2,1)} %get-tuple-element.109), calls=%async_computation.2 | async-start | bytes 655360 | tf_op jit(solution)/shard_map/all_to_all | solution.py:1096
  116.2 210.3 %reduce-scatter.2.cloned.1.call-start = ((), (), s32[]{:S(2)}) async-start(), calls=%async_computation.7 | async-start | bytes 10948608 | tf_op jit(solution)/shard_map/reduce_scatter | solution.py:1287
  176.2 18.2 %all-to-all-start.3 = ((bf16[32,32,128]{2,1,0:T(8,128)(2,1)}), bf16[32,32,128]{2,1,0:T(8,128)(2,1)S(1)}, u32[]{:S(2)}, u32[]{:S(2)}) async-start(bf16[32,32,128]{2,1,0:T(8,128)(2,1)} %get-tuple-element.124), calls=%async_computation.3 | async-start | bytes 524288 | tf_op jit(solution)/shard_map/all_to_all | solution.py:1096
  197.6 22.0 %all-to-all-start.4 = ((bf16[32,40,128]{2,1,0:T(8,128)(2,1)}), bf16[32,40,128]{2,1,0:T(8,128)(2,1)S(1)}, u32[]{:S(2)}, u32[]{:S(2)}) async-start(bf16[32,40,128]{2,1,0:T(8,128)(2,1)} %get-tuple-element.129), calls=%async_computation.4 | async-start | bytes 655360 | tf_op jit(solution)/shard_map/all_to_all | solution.py:1096
  228.9 25.5 %all-to-all-start.5 = ((bf16[32,8,768]{2,1,0:T(8,128)(2,1)}), bf16[32,8,768]{2,1,0:T(8,128)(2,1)S(1)}, u32[]{:S(2)}, u32[]{:S(2)}) async-start(bf16[32,8,768]{2,1,0:T(8,128)(2,1)} %get-tuple-element.137), calls=%async_computation.5 | async-start | bytes 786432 | tf_op jit(solution)/shard_map/all_to_all | solution.py:1096
  270.7 19.3 %collective-permute-start.15 = (bf16[8,32,768]{2,1,0:T(8,128)(2,1)}, bf16[8,32,768]{2,1,0:T(8,128)(2,1)S(1)}, u32[]{:S(2)}, u32[]{:S(2)}) collective-permute-start(bf16[8,32,768]{2,1,0:T(8,128)(2,1)} %get-tuple-element.158), channel_id=1, source_target_pairs={{0,2},{1,3},{2,0},{3,1},{4,6},{5,7},{6,4},{7,5},{8,10},{9,11},{10,... | collective-permute-start | bytes 1179656 | tf_op jit(solution)/shard_map/ppermute | solution.py:190
  273.1 11.5 %collective-permute-start.16 = (bf16[8,24,768]{2,1,0:T(8,128)(2,1)}, bf16[8,24,768]{2,1,0:T(8,128)(2,1)S(1)}, u32[]{:S(2)}, u32[]{:S(2)}) collective-permute-start(bf16[8,24,768]{2,1,0:T(8,128)(2,1)} %get-tuple-element.160), channel_id=1, source_target_pairs={{0,4},{1,5},{2,6},{3,7},{4,0},{5,1},{6,2},{7,3},{8,12},{9,13},{10,... | collective-permute-start | bytes 884744 | tf_op jit(solution)/shard_map/ppermute | solution.py:190
  274.7 15.3 %collective-permute-start.17 = (bf16[8,24,768]{2,1,0:T(8,128)(2,1)}, bf16[8,24,768]{2,1,0:T(8,128)(2,1)S(1)}, u32[]{:S(2)}, u32[]{:S(2)}) collective-permute-start(bf16[8,24,768]{2,1,0:T(8,128)(2,1)} %get-tuple-element.162), channel_id=1, source_target_pairs={{0,8},{1,9},{2,10},{3,11},{4,12},{5,13},{6,14},{7,15},{8,0},{9,1},... | collective-permute-start | bytes 884744 | tf_op jit(solution)/shard_map/ppermute | solution.py:190
  293.5 11.8 %collective-permute-start.18 = (bf16[4,32,768]{2,1,0:T(8,128)(2,1)S(1)}, bf16[4,32,768]{2,1,0:T(8,128)(2,1)S(1)}, u32[]{:S(2)}, u32[]{:S(2)}) collective-permute-start(bf16[4,32,768]{2,1,0:T(8,128)(2,1)S(1)} %get-tuple-element.164), channel_id=1, source_target_pairs={{0,4},{1,5},{2,6},{3,7},{4,0},{5,1},{6,2},{7,3},{8,12},{9,13},{10,... | collective-permute-start | bytes 589832 | tf_op jit(solution)/shard_map/ppermute | solution.py:190
  293.6 5.2 %collective-permute-start.19 = (bf16[4,24,768]{2,1,0:T(8,128)(2,1)S(1)}, bf16[4,24,768]{2,1,0:T(8,128)(2,1)S(1)}, u32[]{:S(2)}, u32[]{:S(2)}) collective-permute-start(bf16[4,24,768]{2,1,0:T(8,128)(2,1)S(1)} %get-tuple-element.166), channel_id=1, source_target_pairs={{0,2},{1,3},{2,0},{3,1},{4,6},{5,7},{6,4},{7,5},{8,10},{9,11},{10,... | collective-permute-start | bytes 442376 | tf_op jit(solution)/shard_map/ppermute | solution.py:190
  293.7 11.6 %collective-permute-start.20 = (bf16[4,24,768]{2,1,0:T(8,128)(2,1)S(1)}, bf16[4,24,768]{2,1,0:T(8,128)(2,1)S(1)}, u32[]{:S(2)}, u32[]{:S(2)}) collective-permute-start(bf16[4,24,768]{2,1,0:T(8,128)(2,1)S(1)} %get-tuple-element.168), channel_id=1, source_target_pairs={{0,24},{1,25},{2,26},{3,27},{4,28},{5,29},{6,30},{7,31},{8,16},{9,... | collective-permute-start | bytes 442376 | tf_op jit(solution)/shard_map/ppermute | solution.py:190
  305.4 6.4 %collective-permute-start.21 = (bf16[2,56,768]{2,1,0:T(8,128)(2,1)S(1)}, bf16[2,56,768]{2,1,0:T(8,128)(2,1)S(1)}, u32[]{:S(2)}, u32[]{:S(2)}) collective-permute-start(bf16[2,56,768]{2,1,0:T(8,128)(2,1)S(1)} %get-tuple-element.170), channel_id=1, source_target_pairs={{0,8},{1,9},{2,10},{3,11},{4,12},{5,13},{6,14},{7,15},{8,0},{9,1},... | collective-permute-start | bytes 516104 | tf_op jit(solution)/shard_map/ppermute | solution.py:190
  311.9 7.2 %collective-permute-start.23 = (bf16[1,56,768]{2,1,0:T(8,128)(2,1)S(1)}, bf16[1,56,768]{2,1,0:T(8,128)(2,1)S(1)}, u32[]{:S(2)}, u32[]{:S(2)}) collective-permute-start(bf16[1,56,768]{2,1,0:T(8,128)(2,1)S(1)} %get-tuple-element.174), channel_id=1, source_target_pairs={{0,24},{1,25},{2,26},{3,27},{4,28},{5,29},{6,30},{7,31},{8,16},{9,... | collective-permute-start | bytes 258056 | tf_op jit(solution)/shard_map/ppermute | solution.py:190
  (29 other events, 94.1 us)
Sparse Core Ops, SparseCore 0:
  20.2 99.7 all-gather.2
  169.7 156.8 reduce-scatter.1

commit v2 on v1

--- a/solution.py
+++ b/solution.py
@@ -370,15 +370,17 @@
     lax.fori_loop(0, n // 2, place_rows, 0)
 
 
-def query_key_kernel(cfg, me_ref, x_ref, *refs):
+def query_key_kernel(cfg, me_ref, *refs):
     n, core, hyper, rows, parts, scale, segment, heads_dev, head_size = cfg
-    ins, refs = refs[:4], refs[4:]
+    ins, x_ref, refs = refs[:4], refs[4], refs[5:]
     q_ref, k_ref, land_ref, wqk = refs
     me = me_ref[0]
     width = x_ref.shape[1]
-    ready(*ins)
     if hyper:
-        natural(ins, ((0, wqk.buf.at[0]), (1, wqk.buf.at[1])), me, n, core, rows, width)
+        for ref in ins:
+            ref.ready(0)
+        bufs = [ref.buf for ref in ins]
+        natural(bufs, ((0, wqk.buf.at[0]), (1, wqk.buf.at[1])), me, n, core, rows, width)
     else:
         for unit, piece in enumerate(ins[:2]):
             wqk[unit] = piece[...]
@@ -521,7 +523,7 @@
         out[1] = jnp.where(second, wide, 0.0)
 
 
-def score3_kernel(heads, parts, k_ref, v_ref, got_ref, ql_ref, kl_ref, p_ref, out_ref, lands):
+def score3_kernel(heads, parts, got_ref, k_ref, v_ref, ql_ref, kl_ref, p_ref, out_ref, lands):
     tokens = k_ref.shape[0] // 2
     n = out_ref.shape[0]
     width = k_ref.shape[1]
@@ -1168,14 +1170,19 @@
     weight = shape_of((width, width), bf16)
     weight_full = shape_of((width, width), f32)
     toeplitz = shape_of((heads, CT, CE), bf16)
+    piece_parts = None
+    if hyper:
+        spans = (slice(0, 2 * rows), slice(2 * rows, None))
+        piece_parts = {i: [(slice(None), span) for span in spans] for i in range(4)}
     queries, keys, lands, wqk = vmem_call(
         functools.partial(query_key_kernel, cfg),
         (
             square_low, square_low, shape_of((n, 8, width), bf16 if held >= segment else f32),
             shape_of((2, width, width), bf16),
         ),
-        (me, x, *pieces),
+        (me, *pieces, x),
         scalars=1,
+        parts=piece_parts,
     )
     lands = exchange(lands)
     values, toep, peot, gains, wv = vmem_call(
@@ -1201,7 +1208,7 @@
     q_land, k_land, p3, sent = vmem_call(
         functools.partial(score3_kernel, heads, parts),
         (land, land, shape_of((2, groups, GW, held), bf16), slots),
-        (keys, values, lands),
+        (lands, keys, values),
         scratch=[pltpu.VMEM((4, n * parts, width), f32)],
     )
     got_sums = exchange(sent)

time: 336 us -> 337 us (level)
  no operation moved by 1% of the time
where the time goes in v2:
time: 337 us; the launch traced here: 336 us
  Pallas kernels  146 us (43%)
  waiting for transfers between devices  102 us (30%)
  starting transfers between devices  55.8 us (17%)
  between operations  14.5 us (4%)
  local copies, waits for them, and re-layouts  14.4 us (4%)
  other arithmetic  3.51 us (1%)
    pallas_call x18, Pallas kernels, vmem_call(): pl.pallas_call(run, out_shape=outs, in_specs=[pl.BlockSpec(memory_space=p...  145 us
    ppermute x21, waiting for transfers between devices, swap(): return lax.ppermute(x, AX, [(i, i ^ mask) for i in range(n)])  65.3 us
    all_to_all x6, waiting for transfers between devices, exchange(): return lax.all_to_all(x, AX, 0, 0, tiled=True)  30.2 us
    all_to_all x6, starting transfers between devices, exchange(): return lax.all_to_all(x, AX, 0, 0, tiled=True)  27.3 us
    ppermute x21, starting transfers between devices, swap(): return lax.ppermute(x, AX, [(i, i ^ mask) for i in range(n)])  19.8 us
    unnamed x40, local copies, waits for them, and re-layouts  8.69 us
  transfers between devices with their start and end apart: 33, of which 24 were waited for; matrix products, arithmetic and copies ran while one was open for 2% of the time, Pallas kernels for 30%

profile of v2, /device:TPU:0, one launch (start us, length us, event | category | flops | bytes accessed | tf_op | source)
XLA Modules:
  0.0 335.8 jit_solution(7320672896868250326)
XLA Ops:
  31.7 5.7 %collective-permute-done.2 = bf16[4,80,384]{2,1,0:T(8,128)(2,1)S(1)} collective-permute-done((bf16[4,80,384]{2,1,0:T(8,128)(2,1)S(1)}, bf16[4,80,384]{2,1,0:T(8,128)(2,1)S(1)}, u32[]{:S(2)}, u32[]{:S(2)}) %collective-permute-start.2) | collective-permute-done | bytes 245792 | tf_op jit(solution)/shard_map/ppermute | solution.py:190
  40.7 8.5 %collective-permute-done.3 = bf16[8,80,384]{2,1,0:T(8,128)(2,1)S(1)} collective-permute-done((bf16[8,80,384]{2,1,0:T(8,128)(2,1)S(1)}, bf16[8,80,384]{2,1,0:T(8,128)(2,1)S(1)}, u32[]{:S(2)}, u32[]{:S(2)}) %collective-permute-start.3) | collective-permute-done | bytes 491552 | tf_op jit(solution)/shard_map/ppermute | solution.py:190
  53.6 5.7 %shard_map.195 = (bf16[768,768]{1,0:T(8,128)(2,1)}, bf16[768,768]{1,0:T(8,128)(2,1)}, bf16[32,8,768]{2,1,0:T(8,128)(2,1)}, bf16[2,768,768]{2,1,0:T(8,128)(2,1)}) custom-call(s32[1]{0:T(128)} %bitcast.refs_0_, bf16[16,80,384]{2,1,0:T(8,128)(2,1)} %copy-done.3, bf16[16,80,384]{2,1,0:T(8,128)(2,1)} %copy-done.4, bf16[16,80,384]{2,1,0:T(8,128)(2,1)} %copy-done.5, ...), custom_call_target="tpu_custom_call" | custom-call | tf_op jit(solution)/shard_map/pallas_call | solution.py:151
  63.0 8.4 %shard_map.196 = (bf16[768,768]{1,0:T(8,128)(2,1)}, bf16[12,128,160]{2,1,0:T(8,128)(2,1)}, bf16[12,128,160]{2,1,0:T(8,128)(2,1)}, f32[8,768]{1,0:T(8,128)}, bf16[768,768]{1,0:T(8,128)(2,1)}) custom-call(s32[1]{0:T(128)} %bitcast.refs_0_, bf16[768,768]{1,0:T(8,128)(2,1)} %bitcast.21, bf16[16,80,384]{2,1,0:T(8,128)(2,1)} %copy-done.3, ...), custom_call_target="tpu_custom_call" | custom-call | tf_op jit(solution)/shard_map/pallas_call | solution.py:151
  71.3 7.0 %all-to-all-done.refs_0_ = bf16[32,8,768]{2,1,0:T(8,128)(2,1)S(1)} async-done(((bf16[32,8,768]{2,1,0:T(8,128)(2,1)}), bf16[32,8,768]{2,1,0:T(8,128)(2,1)S(1)}, u32[]{:S(2)}, u32[]{:S(2)}) %all-to-all-start) | async-done | bytes 393248 | tf_op jit(solution)/shard_map/all_to_all | solution.py:1098
  79.0 6.8 %shard_map.197 = (bf16[128,768]{1,0:T(8,128)(2,1)}, bf16[128,768]{1,0:T(8,128)(2,1)}, bf16[2,3,256,384]{3,2,1,0:T(8,128)(2,1)}, bf16[32,40,128]{2,1,0:T(8,128)(2,1)}) custom-call(bf16[32,8,768]{2,1,0:T(8,128)(2,1)} %copy-done.8, bf16[768,768]{1,0:T(8,128)(2,1)} %get-tuple-element.102.refs_1_.refs_4_, ...), custom_call_target="tpu_custom_call" | custom-call | tf_op jit(solution)/shard_map/pallas_call | solution.py:151
  93.6 6.8 %shard_map.198 = (f32[64,64]{1,0:T(8,128)}, f32[6,5,64,64]{3,2,1,0:T(8,128)}, f32[4,64,64]{2,1,0:T(8,128)}) custom-call(s32[1]{0:T(128)} %bitcast.refs_0_, bf16[128,768]{1,0:T(8,128)(2,1)} %get-tuple-element.106.refs_1_.refs_6_, bf16[128,768]{1,0:T(8,128)(2,1)} %get-tuple-element.107.refs_2_.refs_4_.refs_3_), custom_call_target="tpu_custom_call" | custom-call | tf_op jit(solution)/shard_map/pallas_call | solution.py:151
  100.5 7.3 %all-to-all-done.1.refs_0_ = bf16[32,40,128]{2,1,0:T(8,128)(2,1)S(1)} async-done(((bf16[32,40,128]{2,1,0:T(8,128)(2,1)}), bf16[32,40,128]{2,1,0:T(8,128)(2,1)S(1)}, u32[]{:S(2)}, u32[]{:S(2)}) %all-to-all-start.1) | async-done | bytes 327712 | tf_op jit(solution)/shard_map/all_to_all | solution.py:1098
  111.2 5.6 %all-to-all-start.2 = ((bf16[32,40,128]{2,1,0:T(8,128)(2,1)}), bf16[32,40,128]{2,1,0:T(8,128)(2,1)S(1)}, u32[]{:S(2)}, u32[]{:S(2)}) async-start(bf16[32,40,128]{2,1,0:T(8,128)(2,1)} %get-tuple-element.109), calls=%async_computation.2 | async-start | bytes 655360 | tf_op jit(solution)/shard_map/all_to_all | solution.py:1098
  116.8 6.1 %shard_map.200 = (f32[768,768]{1,0:T(8,128)}, bf16[2,3,256,384]{3,2,1,0:T(8,128)(2,1)}) custom-call(bf16[768,768]{1,0:T(8,128)(2,1)} %get-tuple-element.110.refs_0_.refs_4_, bf16[768,768]{1,0:T(8,128)(2,1)} %get-tuple-element.103.refs_2_.refs_1_.refs_3_.refs_5_, bf16[2,16,768]{2,1,0:T(8,128)(2,1)} %copy-done.16, bf16[2,16,768]{2,1,0:T(8,128)(2,1)} %copy-done.15, ...), custom_call_target="tpu_custom_call" | custom-call | tf_op jit(solution)/shard_map/pallas_call | solution.py:151
  122.9 5.8 %all-to-all-done.2.refs_2_.refs_1_ = bf16[32,40,128]{2,1,0:T(8,128)(2,1)S(1)} async-done(((bf16[32,40,128]{2,1,0:T(8,128)(2,1)}), bf16[32,40,128]{2,1,0:T(8,128)(2,1)S(1)}, u32[]{:S(2)}, u32[]{:S(2)}) %all-to-all-start.2) | async-done | bytes 327712 | tf_op jit(solution)/shard_map/all_to_all | solution.py:1098
  129.5 40.6 %shard_map.201 = (bf16[2,3,256,256]{3,2,1,0:T(8,128)(2,1)}, bf16[768,768]{1,0:T(8,128)(2,1)}, f32[768,768]{1,0:T(8,128)}, bf16[768,768]{1,0:T(8,128)(2,1)}, f32[...) custom-call(bf16[2,3,256,384]{3,2,1,0:T(8,128)(2,1)} %get-tuple-element.115.refs_0_.refs_1_, ...), custom_call_target="tpu_custom_call" | custom-call | tf_op jit(solution)/shard_map/pallas_call | solution.py:151
  170.1 6.7 %shard_map.202 = (f32[768,768]{1,0:T(8,128)}, f32[2,64,768]{2,1,0:T(8,128)}, bf16[32,32,128]{2,1,0:T(8,128)(2,1)}) custom-call(bf16[768,768]{1,0:T(8,128)(2,1)} %get-tuple-element.122.refs_0_, bf16[2,3,256,384]{3,2,1,0:T(8,128)(2,1)} %get-tuple-element.115.refs_0_.refs_1_, bf16[2,3,256,256]{3,2,1,0:T(8,128)(2,1)} %get-tuple-element.123.refs_2_, ...), custom_call_target="tpu_custom_call" | custom-call | tf_op jit(solution)/shard_map/pallas_call | solution.py:151
  186.3 8.7 %shard_map.203 = (f32[768,768]{1,0:T(8,128)}, f32[3,4,256]{2,1,0:T(4,128)}) custom-call(bf16[768,768]{1,0:T(8,128)(2,1)} %get-tuple-element.122.refs_0_, bf16[2,16,768]{2,1,0:T(8,128)(2,1)} %copy-done.18, bf16[2,16,768]{2,1,0:T(8,128)(2,1)} %copy-done.17, bf16[768,768]{1,0:T(8,128)(2,1)} %get-tuple-element.103.refs_2_.refs_1_.refs_3_.refs_5_, ...), custom_call_target="tpu_custom_call" | custom-call | tf_op jit(solution)/shard_map/pallas_call | solution.py:151
  198.2 10.0 %all-to-all-start.4 = ((bf16[32,40,128]{2,1,0:T(8,128)(2,1)}), bf16[32,40,128]{2,1,0:T(8,128)(2,1)S(1)}, u32[]{:S(2)}, u32[]{:S(2)}) async-start(bf16[32,40,128]{2,1,0:T(8,128)(2,1)} %get-tuple-element.129), calls=%async_computation.4 | async-start | bytes 655360 | tf_op jit(solution)/shard_map/all_to_all | solution.py:1098
  208.2 8.8 %shard_map.205 = (f32[2,64,768]{2,1,0:T(8,128)}, f32[2,64,768]{2,1,0:T(8,128)}) custom-call(s32[1]{0:T(128)} %bitcast.refs_0_, f32[64,64]{1,0:T(8,128)} %get-tuple-element.131.refs_1_, f32[64,64]{1,0:T(8,128)} %get-tuple-element.108.refs_1_.refs_2_, f32[6,5,64,64]{3,2,1,0:T(8,128)} %get-tuple-element.132.refs_3_, f32[4,64,64]{2,1,0:T(8,128)} %get-tuple-element.133.refs_4_), custom_call_target="tpu_custom_call" | custom-call | tf_op jit(solution)/shard_map/pallas_call | solution.py:151
  220.9 8.5 %shard_map.206 = (f32[768,768]{1,0:T(8,128)}, f32[768,768]{1,0:T(8,128)}, bf16[32,8,768]{2,1,0:T(8,128)(2,1)}) custom-call(bf16[32,40,128]{2,1,0:T(8,128)(2,1)} %get-tuple-element.104.refs_0_, bf16[32,40,128]{2,1,0:T(8,128)(2,1)} %copy-done.7, bf16[32,40,128]{2,1,0:T(8,128)(2,1)} %copy-done.9, bf16[2,3,256,384]{3,2,1,0:T(8,128)(2,1)} %get-tuple-element.130.refs_3_, ...), custom_call_target="tpu_custom_call" | custom-call | tf_op jit(solution)/shard_map/pallas_call | solution.py:151
  234.1 14.9 %shard_map.207 = (f32[768,768]{1,0:T(8,128)}, f32[8,768]{1,0:T(8,128)}, f32[2,768,768]{2,1,0:T(8,128)}, bf16[16,24,768]{2,1,0:T(8,128)(2,1)}, bf16[16,24,768]{2,1,0:T(8,128)(2,1)}) custom-call(s32[1]{0:T(128)} %bitcast.refs_0_, bf16[768,768]{1,0:T(8,128)(2,1)} %bitcast.23, f32[768,768]{1,0:T(8,128)} %get-tuple-element.138.refs_2_, ...), custom_call_target="tpu_custom_call" | custom-call | tf_op jit(solution)/shard_map/pallas_call | solution.py:151
  249.0 6.9 %all-to-all-done.5.refs_1_.refs_0_ = bf16[32,8,768]{2,1,0:T(8,128)(2,1)S(1)} async-done(((bf16[32,8,768]{2,1,0:T(8,128)(2,1)}), bf16[32,8,768]{2,1,0:T(8,128)(2,1)S(1)}, u32[]{:S(2)}, u32[]{:S(2)}) %all-to-all-start.5) | async-done | bytes 393248 | tf_op jit(solution)/shard_map/all_to_all | solution.py:1098
  256.7 6.1 %shard_map.208 = (bf16[16,32,768]{2,1,0:T(8,128)(2,1)}, bf16[16,32,768]{2,1,0:T(8,128)(2,1)}, bf16[16,24,768]{2,1,0:T(8,128)(2,1)}, bf16[16,24,768]{2,1,0:T(8,128)(2,1)}) custom-call(s32[1]{0:T(128)} %bitcast.refs_0_, bf16[32,8,768]{2,1,0:T(8,128)(2,1)} %copy-done.6, f32[8,768]{1,0:T(8,128)} %get-tuple-element.145.refs_2_, ...), custom_call_target="tpu_custom_call" | custom-call | tf_op jit(solution)/shard_map/pallas_call | solution.py:151
  275.3 10.0 %collective-permute-done.16.refs_3_ = bf16[8,24,768]{2,1,0:T(8,128)(2,1)S(1)} collective-permute-done((bf16[8,24,768]{2,1,0:T(8,128)(2,1)}, bf16[8,24,768]{2,1,0:T(8,128)(2,1)S(1)}, u32[]{:S(2)}, u32[]{:S(2)}) %collective-permute-start.16) | collective-permute-done | bytes 294944 | tf_op jit(solution)/shard_map/ppermute | solution.py:190
  285.3 5.3 %collective-permute-done.17.refs_5_ = bf16[8,24,768]{2,1,0:T(8,128)(2,1)S(1)} collective-permute-done((bf16[8,24,768]{2,1,0:T(8,128)(2,1)}, bf16[8,24,768]{2,1,0:T(8,128)(2,1)S(1)}, u32[]{:S(2)}, u32[]{:S(2)}) %collective-permute-start.17) | collective-permute-done | bytes 294944 | tf_op jit(solution)/shard_map/ppermute | solution.py:190
  299.4 6.5 %collective-permute-done.20.refs_5_ = bf16[4,24,768]{2,1,0:T(8,128)(2,1)S(1)} collective-permute-done((bf16[4,24,768]{2,1,0:T(8,128)(2,1)S(1)}, bf16[4,24,768]{2,1,0:T(8,128)(2,1)S(1)}, u32[]{:S(2)}, u32[]{:S(2)}) %collective-permute-start.20) | collective-permute-done | bytes 147488 | tf_op jit(solution)/shard_map/ppermute | solution.py:190
  321.7 5.4 %reduce-scatter.2.cloned.1.call-done = bf16[1,9,24,768]{3,2,1,0:T(8,128)(2,1)} async-done(((bf16[32,9,24,768]{3,2,1,0:T(8,128)(2,1)}), bf16[1,9,24,768]{3,2,1,0:T(8,128)(2,1)}) %reduce-scatter.2.cloned.1.call-update) | async-done | bytes 331792 | tf_op jit(solution)/shard_map/reduce_scatter | solution.py:1294
  (128 shorter events, 109.1 us)
Async XLA Ops:
  7.2 121.6 %all-gather.3.cloned.1.call-start = ((), (), s32[]{:S(2)}) async-start(), calls=%async_computation.8 | async-start | bytes 10948608 | tf_op jit(solution)/shard_map/all_gather | solution.py:1138
  10.4 8.8 %collective-permute-start = (bf16[1,80,768]{2,1,0:T(8,128)(2,1)}, bf16[1,80,768]{2,1,0:T(8,128)(2,1)S(1)}, u32[]{:S(2)}, u32[]{:S(2)}) collective-permute-start(bf16[1,80,768]{2,1,0:T(8,128)(2,1)} %bitcast.28), channel_id=1, source_target_pairs={{0,24},{1,25},{2,26},{3,27},{4,28},{5,29},{6,30},{7,31},{8,16},{9,... | collective-permute-start | bytes 368648 | tf_op jit(solution)/shard_map/ppermute | solution.py:190
  20.1 7.6 %collective-permute-start.1 = (bf16[2,80,768]{2,1,0:T(8,128)(2,1)S(1)}, bf16[2,80,768]{2,1,0:T(8,128)(2,1)S(1)}, u32[]{:S(2)}, u32[]{:S(2)}) collective-permute-start(bf16[2,80,768]{2,1,0:T(8,128)(2,1)S(1)} %pad_maximum_fusion.5), channel_id=1, source_target_pairs={{0,8},{1,9},{2,10},{3,11},{4,12},{5,13},{6,14},{7,15},{8,0},{9,1},... | collective-permute-start | bytes 737288 | tf_op jit(solution)/shard_map/ppermute | solution.py:190
  28.7 8.8 %collective-permute-start.2 = (bf16[4,80,384]{2,1,0:T(8,128)(2,1)S(1)}, bf16[4,80,384]{2,1,0:T(8,128)(2,1)S(1)}, u32[]{:S(2)}, u32[]{:S(2)}) collective-permute-start(bf16[4,80,384]{2,1,0:T(8,128)(2,1)S(1)} %get-tuple-element.190), channel_id=1, source_target_pairs={{0,4},{1,5},{2,6},{3,7},{4,0},{5,1},{6,2},{7,3},{8,12},{9,13},{10,... | collective-permute-start | bytes 737288 | tf_op jit(solution)/shard_map/ppermute | solution.py:190
  30.2 10.2 %collective-permute-start.4 = (bf16[4,80,384]{2,1,0:T(8,128)(2,1)S(1)}, bf16[4,80,384]{2,1,0:T(8,128)(2,1)S(1)}, u32[]{:S(2)}, u32[]{:S(2)}) collective-permute-start(bf16[4,80,384]{2,1,0:T(8,128)(2,1)S(1)} %get-tuple-element.189), channel_id=1, source_target_pairs={{0,2},{1,3},{2,0},{3,1},{4,6},{5,7},{6,4},{7,5},{8,10},{9,11},{10,... | collective-permute-start | bytes 737288 | tf_op jit(solution)/shard_map/ppermute | solution.py:190
  37.5 11.7 %collective-permute-start.3 = (bf16[8,80,384]{2,1,0:T(8,128)(2,1)S(1)}, bf16[8,80,384]{2,1,0:T(8,128)(2,1)S(1)}, u32[]{:S(2)}, u32[]{:S(2)}) collective-permute-start(bf16[8,80,384]{2,1,0:T(8,128)(2,1)S(1)} %pad_maximum_fusion.3), channel_id=1, source_target_pairs={{0,2},{1,3},{2,0},{3,1},{4,6},{5,7},{6,4},{7,5},{8,10},{9,11},{10,... | collective-permute-start | bytes 1474568 | tf_op jit(solution)/shard_map/ppermute | solution.py:190
  40.5 9.4 %collective-permute-start.5 = (bf16[8,80,384]{2,1,0:T(8,128)(2,1)S(1)}, bf16[8,80,384]{2,1,0:T(8,128)(2,1)S(1)}, u32[]{:S(2)}, u32[]{:S(2)}) collective-permute-start(bf16[8,80,384]{2,1,0:T(8,128)(2,1)S(1)} %pad_maximum_fusion.4), channel_id=1, source_target_pairs={{0,4},{1,5},{2,6},{3,7},{4,0},{5,1},{6,2},{7,3},{8,12},{9,13},{10,... | collective-permute-start | bytes 1474568 | tf_op jit(solution)/shard_map/ppermute | solution.py:190
  59.3 19.0 %all-to-all-start = ((bf16[32,8,768]{2,1,0:T(8,128)(2,1)}), bf16[32,8,768]{2,1,0:T(8,128)(2,1)S(1)}, u32[]{:S(2)}, u32[]{:S(2)}) async-start(bf16[32,8,768]{2,1,0:T(8,128)(2,1)} %get-tuple-element.99), calls=%async_computation | async-start | bytes 786432 | tf_op jit(solution)/shard_map/all_to_all | solution.py:1098
  85.9 22.0 %all-to-all-start.1 = ((bf16[32,40,128]{2,1,0:T(8,128)(2,1)}), bf16[32,40,128]{2,1,0:T(8,128)(2,1)S(1)}, u32[]{:S(2)}, u32[]{:S(2)}) async-start(bf16[32,40,128]{2,1,0:T(8,128)(2,1)} %get-tuple-element.104.refs_0_), calls=%async_computation.1 | async-start | bytes 655360 | tf_op jit(solution)/shard_map/all_to_all | solution.py:1098
  89.3 11.2 %collective-permute-start.9 = (bf16[2,16,768]{2,1,0:T(8,128)(2,1)S(1)}, bf16[2,16,768]{2,1,0:T(8,128)(2,1)S(1)}, u32[]{:S(2)}, u32[]{:S(2)}) collective-permute-start(bf16[2,16,768]{2,1,0:T(8,128)(2,1)S(1)} %get-tuple-element.187), channel_id=1, source_target_pairs={{1,0},{2,1},{3,2},{4,3},{5,4},{6,5},{7,6},{8,7},{9,8},{10,9},{11,1... | collective-permute-start | bytes 147464 | tf_op jit(solution)/shard_map/ppermute | solution.py:1201
  90.6 9.9 %collective-permute-start.8 = (bf16[2,16,768]{2,1,0:T(8,128)(2,1)S(1)}, bf16[2,16,768]{2,1,0:T(8,128)(2,1)S(1)}, u32[]{:S(2)}, u32[]{:S(2)}) collective-permute-start(bf16[2,16,768]{2,1,0:T(8,128)(2,1)S(1)} %get-tuple-element.188), channel_id=1, source_target_pairs={{0,1},{1,2},{2,3},{3,4},{4,5},{5,6},{6,7},{7,8},{8,9},{9,10},{10,1... | collective-permute-start | bytes 147464 | tf_op jit(solution)/shard_map/ppermute | solution.py:1200
  111.2 17.6 %all-to-all-start.2 = ((bf16[32,40,128]{2,1,0:T(8,128)(2,1)}), bf16[32,40,128]{2,1,0:T(8,128)(2,1)S(1)}, u32[]{:S(2)}, u32[]{:S(2)}) async-start(bf16[32,40,128]{2,1,0:T(8,128)(2,1)} %get-tuple-element.109), calls=%async_computation.2 | async-start | bytes 655360 | tf_op jit(solution)/shard_map/all_to_all | solution.py:1098
  116.8 210.4 %reduce-scatter.2.cloned.1.call-start = ((), (), s32[]{:S(2)}) async-start(), calls=%async_computation.7 | async-start | bytes 10948608 | tf_op jit(solution)/shard_map/reduce_scatter | solution.py:1294
  176.8 18.2 %all-to-all-start.3 = ((bf16[32,32,128]{2,1,0:T(8,128)(2,1)}), bf16[32,32,128]{2,1,0:T(8,128)(2,1)S(1)}, u32[]{:S(2)}, u32[]{:S(2)}) async-start(bf16[32,32,128]{2,1,0:T(8,128)(2,1)} %get-tuple-element.124), calls=%async_computation.3 | async-start | bytes 524288 | tf_op jit(solution)/shard_map/all_to_all | solution.py:1098
  198.2 22.0 %all-to-all-start.4 = ((bf16[32,40,128]{2,1,0:T(8,128)(2,1)}), bf16[32,40,128]{2,1,0:T(8,128)(2,1)S(1)}, u32[]{:S(2)}, u32[]{:S(2)}) async-start(bf16[32,40,128]{2,1,0:T(8,128)(2,1)} %get-tuple-element.129), calls=%async_computation.4 | async-start | bytes 655360 | tf_op jit(solution)/shard_map/all_to_all | solution.py:1098
  229.5 26.4 %all-to-all-start.5 = ((bf16[32,8,768]{2,1,0:T(8,128)(2,1)}), bf16[32,8,768]{2,1,0:T(8,128)(2,1)S(1)}, u32[]{:S(2)}, u32[]{:S(2)}) async-start(bf16[32,8,768]{2,1,0:T(8,128)(2,1)} %get-tuple-element.137), calls=%async_computation.5 | async-start | bytes 786432 | tf_op jit(solution)/shard_map/all_to_all | solution.py:1098
  272.2 18.4 %collective-permute-start.15 = (bf16[8,32,768]{2,1,0:T(8,128)(2,1)}, bf16[8,32,768]{2,1,0:T(8,128)(2,1)S(1)}, u32[]{:S(2)}, u32[]{:S(2)}) collective-permute-start(bf16[8,32,768]{2,1,0:T(8,128)(2,1)} %get-tuple-element.158), channel_id=1, source_target_pairs={{0,2},{1,3},{2,0},{3,1},{4,6},{5,7},{6,4},{7,5},{8,10},{9,11},{10,... | collective-permute-start | bytes 1179656 | tf_op jit(solution)/shard_map/ppermute | solution.py:190
  273.7 11.6 %collective-permute-start.16 = (bf16[8,24,768]{2,1,0:T(8,128)(2,1)}, bf16[8,24,768]{2,1,0:T(8,128)(2,1)S(1)}, u32[]{:S(2)}, u32[]{:S(2)}) collective-permute-start(bf16[8,24,768]{2,1,0:T(8,128)(2,1)} %get-tuple-element.160), channel_id=1, source_target_pairs={{0,4},{1,5},{2,6},{3,7},{4,0},{5,1},{6,2},{7,3},{8,12},{9,13},{10,... | collective-permute-start | bytes 884744 | tf_op jit(solution)/shard_map/ppermute | solution.py:190
  275.3 15.3 %collective-permute-start.17 = (bf16[8,24,768]{2,1,0:T(8,128)(2,1)}, bf16[8,24,768]{2,1,0:T(8,128)(2,1)S(1)}, u32[]{:S(2)}, u32[]{:S(2)}) collective-permute-start(bf16[8,24,768]{2,1,0:T(8,128)(2,1)} %get-tuple-element.162), channel_id=1, source_target_pairs={{0,8},{1,9},{2,10},{3,11},{4,12},{5,13},{6,14},{7,15},{8,0},{9,1},... | collective-permute-start | bytes 884744 | tf_op jit(solution)/shard_map/ppermute | solution.py:190
  294.1 11.8 %collective-permute-start.18 = (bf16[4,32,768]{2,1,0:T(8,128)(2,1)S(1)}, bf16[4,32,768]{2,1,0:T(8,128)(2,1)S(1)}, u32[]{:S(2)}, u32[]{:S(2)}) collective-permute-start(bf16[4,32,768]{2,1,0:T(8,128)(2,1)S(1)} %get-tuple-element.164), channel_id=1, source_target_pairs={{0,4},{1,5},{2,6},{3,7},{4,0},{5,1},{6,2},{7,3},{8,12},{9,13},{10,... | collective-permute-start | bytes 589832 | tf_op jit(solution)/shard_map/ppermute | solution.py:190
  294.2 5.2 %collective-permute-start.19 = (bf16[4,24,768]{2,1,0:T(8,128)(2,1)S(1)}, bf16[4,24,768]{2,1,0:T(8,128)(2,1)S(1)}, u32[]{:S(2)}, u32[]{:S(2)}) collective-permute-start(bf16[4,24,768]{2,1,0:T(8,128)(2,1)S(1)} %get-tuple-element.166), channel_id=1, source_target_pairs={{0,2},{1,3},{2,0},{3,1},{4,6},{5,7},{6,4},{7,5},{8,10},{9,11},{10,... | collective-permute-start | bytes 442376 | tf_op jit(solution)/shard_map/ppermute | solution.py:190
  294.3 11.7 %collective-permute-start.20 = (bf16[4,24,768]{2,1,0:T(8,128)(2,1)S(1)}, bf16[4,24,768]{2,1,0:T(8,128)(2,1)S(1)}, u32[]{:S(2)}, u32[]{:S(2)}) collective-permute-start(bf16[4,24,768]{2,1,0:T(8,128)(2,1)S(1)} %get-tuple-element.168), channel_id=1, source_target_pairs={{0,24},{1,25},{2,26},{3,27},{4,28},{5,29},{6,30},{7,31},{8,16},{9,... | collective-permute-start | bytes 442376 | tf_op jit(solution)/shard_map/ppermute | solution.py:190
  306.1 6.4 %collective-permute-start.21 = (bf16[2,56,768]{2,1,0:T(8,128)(2,1)S(1)}, bf16[2,56,768]{2,1,0:T(8,128)(2,1)S(1)}, u32[]{:S(2)}, u32[]{:S(2)}) collective-permute-start(bf16[2,56,768]{2,1,0:T(8,128)(2,1)S(1)} %get-tuple-element.170), channel_id=1, source_target_pairs={{0,8},{1,9},{2,10},{3,11},{4,12},{5,13},{6,14},{7,15},{8,0},{9,1},... | collective-permute-start | bytes 516104 | tf_op jit(solution)/shard_map/ppermute | solution.py:190
  312.5 7.1 %collective-permute-start.23 = (bf16[1,56,768]{2,1,0:T(8,128)(2,1)S(1)}, bf16[1,56,768]{2,1,0:T(8,128)(2,1)S(1)}, u32[]{:S(2)}, u32[]{:S(2)}) collective-permute-start(bf16[1,56,768]{2,1,0:T(8,128)(2,1)S(1)} %get-tuple-element.174), channel_id=1, source_target_pairs={{0,24},{1,25},{2,26},{3,27},{4,28},{5,29},{6,30},{7,31},{8,16},{9,... | collective-permute-start | bytes 258056 | tf_op jit(solution)/shard_map/ppermute | solution.py:190
  (29 other events, 95.4 us)
Sparse Core Ops, SparseCore 0:
  20.2 100.6 all-gather.2
  170.2 156.8 reduce-scatter.1
